TPU v7x, 128 devices: a whole 4x4x4 slice. The times are simulated.
128 devices in a mesh: chord: 4 (over x_lo, core), normal: 32 (over x_hi, y, z).
Axes of the slice: x: 4 (x_hi: 2, x_lo: 2; x = x_hi * 2 + x_lo), y: 4, z: 4, core: 2. Of those that a mesh axis runs over, the one named last changes fastest.
Arguments:
- direct_modes: bfloat16 [16, 5, 64, 512, 256], P(None, None, 'chord', 'normal'), may hold values from -62 to 62
- adjoint_modes: bfloat16 [16, 5, 64, 512, 256], P(None, None, 'chord', 'normal'), may hold values from -5 to 5
- base_flow: float32 [5, 64, 512, 256], P(None, 'chord', 'normal'), may hold values from -5 to 5
- cell_type: int32 [64, 512, 256], P('chord', 'normal'), may hold values from 0 to 2
- mode_pick: int32 [16], replicated, may hold values from 0 to 15, each once
- flux_mix: float32 [3, 5, 5], replicated, may hold values from -2.5 to 2.5
Outputs:
- sensitivity: float32 [5, 64, 512, 256], P(None, 'chord', 'normal')
Inputs may be any that keep to these rules, and one draw needn't show every extreme that they name: `mode_pick`: each mode once.
All inputs are finite; a program needn't handle non-finite values.
Results may differ from a plain program's by a relative error of at most 0.0003.
Values may be sent and summed in bfloat16 or wider, within the bound.
A program may use at most 256 MiB of HBM per device.

v0:
```python
import jax
import jax.numpy as jnp
from jax import lax
from jax.sharding import PartitionSpec as P


def with_halo(cells, sides, width):
    for axis, dim in sides:
        count = lax.axis_size(axis)
        ends = count - 1
        head = lax.slice_in_dim(cells, 0, width, axis=dim)
        tail = lax.slice_in_dim(cells, cells.shape[dim] - width, cells.shape[dim], axis=dim)
        cells = jnp.concatenate(
            [
                lax.ppermute(tail, axis, [(i, (i + 1) % count) for i in range(ends)]),
                cells,
                lax.ppermute(head, axis, [((i + 1) % count, i) for i in range(ends)]),
            ],
            axis=dim,
        )
    return cells


def mixing(matrix, field_in):
    return jnp.einsum("ij,i...->j...", matrix, field_in, precision=lax.Precision.HIGHEST)


def diff_chord(padded):
    return padded[..., 2:, 1:-1, :] - padded[..., :-2, 1:-1, :]


def diff_normal(padded):
    return padded[..., 1:-1, 2:, :] - padded[..., 1:-1, :-2, :]


def inner_cells(padded):
    return padded[..., 1:-1, 1:-1, :]


def diff_span(field_in):
    return jnp.roll(field_in, -1, -1) - jnp.roll(field_in, 1, -1)


def bilinear_term(left_pad, right_pad, flux_mix):
    summed = jnp.zeros(inner_cells(left_pad).shape, jnp.float32)
    for axis_num, differ in ((0, diff_chord), (1, diff_normal)):
        mixed_adj = mixing(flux_mix[axis_num], right_pad)
        summed = summed + differ(left_pad) * inner_cells(mixed_adj) - differ(left_pad * mixed_adj)
    left_in = inner_cells(left_pad)
    mixed_adj = mixing(flux_mix[2], inner_cells(right_pad))
    return summed + diff_span(left_in) * mixed_adj - diff_span(left_in * mixed_adj)


def cell_weight(cell_type):
    return jnp.where(cell_type == 0, 1.0, jnp.where(cell_type == 1, 0.5, 0.0)).astype(jnp.float32)


def per_device(direct_modes, adjoint_modes, base_flow, cell_type, mode_pick, flux_mix):
    modes_count = direct_modes.shape[0]
    cells_all = direct_modes[0].size * lax.axis_size("chord") * lax.axis_size("normal")
    local_sums = jnp.sum(jnp.square(direct_modes.astype(jnp.float32)), axis=(1, 2, 3, 4))
    energy = lax.psum(local_sums, ("chord", "normal")) / cells_all
    amplitude = lax.rsqrt(energy + 1e-06)
    zeros_field = jnp.zeros(base_flow.shape, jnp.float32)
    direct_pad, adjoint_pad = (
        with_halo(direct_modes, (("chord", 2), ("normal", 3)), 1),
        with_halo(adjoint_modes, (("chord", 2), ("normal", 3)), 1),
    )

    def accumulate(number, summed):
        direct = direct_pad[number].astype(jnp.float32)
        adjoint = adjoint_pad[mode_pick[number]].astype(jnp.float32)
        return summed + amplitude[number] * bilinear_term(direct, adjoint, flux_mix)

    gradient = lax.fori_loop(0, modes_count, accumulate, zeros_field) / modes_count
    weight = cell_weight(cell_type)
    base_pad = with_halo(base_flow, (("chord", 1), ("normal", 2)), 1)

    def transpose_step(field_in):
        weighted = with_halo(weight * field_in, (("chord", 1), ("normal", 2)), 1)
        return bilinear_term(base_pad, weighted, flux_mix)

    once_applied = transpose_step(gradient)
    twice_applied = transpose_step(once_applied)
    return twice_applied


def solution(mesh):
    return jax.shard_map(
        per_device,
        mesh=mesh,
        in_specs=(
            P(None, None, "chord", "normal", None),
            P(None, None, "chord", "normal", None),
            P(None, "chord", "normal", None),
            P("chord", "normal", None),
            P(),
            P(),
        ),
        out_specs=P(None, "chord", "normal", None),
        check_vma=False,
    )
```

profile of v0, /device:TPU:6, one launch (start us, length us, event | category | flops | bytes accessed | tf_op | source)
XLA Modules:
  0.0 948.4 jit_solution(10213477555009542439)
XLA Ops:
  29.3 67.5 %psum.7 = f32[16]{0:T(128)S(1)} all-reduce(f32[16]{0:T(128)S(1)} %multiply_reduce_fusion), channel_id=1, replica_groups=mesh['chord'=4,'normal'=32] {'chord','normal'}, use_global_device_ids=true, to_apply=%region_1.0 | all-reduce | flops 16 | bytes 128 | tf_op jit(solution)/shard_map/psum | solution.py:62
  103.6 19.8 %copy_dynamic-update-slice_fusion = bf16[16,5,18,16,256]{4,0,3,2,1:T(8,128)(2,1)} fusion(bf16[16,5,18,16,256]{4,0,3,2,1:T(8,128)(2,1)} %copy_dynamic-update-slice_fusion.4, bf16[16,5,16,16,256]{4,3,2,1,0:T(8,128)(2,1)} %param.9), kind=kLoop, calls=%fused_computation.41 | loop fusion | bytes 20971520
  130.2 8.5 collective-permute-start.9
  140.8 19.5 %copy_dynamic-update-slice_fusion.1 = bf16[16,5,18,16,256]{4,0,3,2,1:T(8,128)(2,1)} fusion(bf16[16,5,18,16,256]{4,0,3,2,1:T(8,128)(2,1)} %copy_dynamic-update-slice_fusion.6, bf16[16,5,16,16,256]{4,3,2,1,0:T(8,128)(2,1)} %param.8), kind=kLoop, calls=%fused_computation.42 | loop fusion | bytes 20971520
  165.9 9.6 %collective-permute-start.5 = (bf16[16,5,18,1,256]{4,0,3,2,1:T(8,128)(2,1)S(1)}, bf16[16,5,18,1,256]{4,0,3,2,1:T(8,128)(2,1)S(1)}, u32[]{:S(2)}, u32[]{:S(2)}) collective-permute-start(bf16[16,5,18,1,256]{4,0,3,2,1:T(8,128)(2,1)S(1)} %get-tuple-element.202), channel_id=1, source_target_pairs={{1,0},{2,1},{3,2},{4,3},{5,4},{6,5},{7,6},{8,7},{9,8},{10,9},{11,1... | collective-permute-start | bytes 2211848 | tf_op jit(solution)/shard_map/ppermute | solution.py:17
  175.5 7.8 pad_maximum_fusion.1
  183.4 13.5 %copy.52 = bf16[16,5,18,18,256]{4,1,3,2,0:T(8,128)(2,1)} copy(bf16[16,5,18,18,256]{4,0,3,2,1:T(8,128)(2,1)S(1)} %pad_maximum_fusion.1) | data formatting | bytes 26542080
  198.7 13.6 %copy.51 = bf16[16,5,18,18,256]{4,1,3,2,0:T(8,128)(2,1)} copy(bf16[16,5,18,18,256]{4,0,3,2,1:T(8,128)(2,1)S(1)} %pad_maximum_fusion) | data formatting | bytes 26542080
  212.3 629.3 %while.14 = (s32[]{:T(128)}, f32[5,16,16,256]{3,0,2,1:T(8,128)}, f32[16]{0:T(128)S(1)}, bf16[16,5,18,18,256]{4,1,3,2,0:T(8,128)(2,1)}, s32[16]{0:T(128)S(1)}, /*...) while((s32[]{:T(128)}, f32[5,16,16,256]{3,0,2,1:T(8,128)}, ...), condition=%wide.region_3.4_spmd.clone, body=%wide.region_2.3_spmd.clone.sunk | while | flops 78295040 | bytes 61221592 | solution.py:75
  229.9 7.6 convert_multiply_fusion.3
  238.2 12.8 %fusion.76 = f32[5,16,16,256]{3,0,2,1:T(8,128)} fusion(f32[5,18,18,256]{3,0,2,1:T(8,128)} %get-tuple-element.300, f32[5,18,18,256]{3,0,2,1:T(8,128)} %copy-done, f32[5,18,18,256]{3,0,2,1:T(8,128)S(1)} %bitcast_convert_fusion.2, f32[5,18,18,256]{3,0,2,1:T(8,128)} %get-tuple-element.301, f32[5,18,18,256]{3,0,2,1:T(8,128)} %get-tuple-element.302, ...), kind=kLoop, calls=%fused_computation.6.clone.1 | loop fusion | flops 6881280 | bytes 22282244 | tf_op jit(solution)/shard_map/while/body/eval_jaxpr/add | solution.py:73
  268.7 7.6 convert_multiply_fusion.3
  277.0 13.4 %fusion.76 = f32[5,16,16,256]{3,0,2,1:T(8,128)} fusion(f32[5,18,18,256]{3,0,2,1:T(8,128)} %get-tuple-element.300, f32[5,18,18,256]{3,0,2,1:T(8,128)} %copy-done, f32[5,18,18,256]{3,0,2,1:T(8,128)S(1)} %bitcast_convert_fusion.2, f32[5,18,18,256]{3,0,2,1:T(8,128)} %get-tuple-element.301, f32[5,18,18,256]{3,0,2,1:T(8,128)} %get-tuple-element.302, ...), kind=kLoop, calls=%fused_computation.6.clone.1 | loop fusion | flops 6881280 | bytes 22282244 | tf_op jit(solution)/shard_map/while/body/eval_jaxpr/add | solution.py:73
  316.3 13.4 %fusion.76 = f32[5,16,16,256]{3,0,2,1:T(8,128)} fusion(f32[5,18,18,256]{3,0,2,1:T(8,128)} %get-tuple-element.300, f32[5,18,18,256]{3,0,2,1:T(8,128)} %copy-done, f32[5,18,18,256]{3,0,2,1:T(8,128)S(1)} %bitcast_convert_fusion.2, f32[5,18,18,256]{3,0,2,1:T(8,128)} %get-tuple-element.301, f32[5,18,18,256]{3,0,2,1:T(8,128)} %get-tuple-element.302, ...), kind=kLoop, calls=%fused_computation.6.clone.1 | loop fusion | flops 6881280 | bytes 22282244 | tf_op jit(solution)/shard_map/while/body/eval_jaxpr/add | solution.py:73
  355.7 13.4 %fusion.76 = f32[5,16,16,256]{3,0,2,1:T(8,128)} fusion(f32[5,18,18,256]{3,0,2,1:T(8,128)} %get-tuple-element.300, f32[5,18,18,256]{3,0,2,1:T(8,128)} %copy-done, f32[5,18,18,256]{3,0,2,1:T(8,128)S(1)} %bitcast_convert_fusion.2, f32[5,18,18,256]{3,0,2,1:T(8,128)} %get-tuple-element.301, f32[5,18,18,256]{3,0,2,1:T(8,128)} %get-tuple-element.302, ...), kind=kLoop, calls=%fused_computation.6.clone.1 | loop fusion | flops 6881280 | bytes 22282244 | tf_op jit(solution)/shard_map/while/body/eval_jaxpr/add | solution.py:73
  395.0 13.4 %fusion.76 = f32[5,16,16,256]{3,0,2,1:T(8,128)} fusion(f32[5,18,18,256]{3,0,2,1:T(8,128)} %get-tuple-element.300, f32[5,18,18,256]{3,0,2,1:T(8,128)} %copy-done, f32[5,18,18,256]{3,0,2,1:T(8,128)S(1)} %bitcast_convert_fusion.2, f32[5,18,18,256]{3,0,2,1:T(8,128)} %get-tuple-element.301, f32[5,18,18,256]{3,0,2,1:T(8,128)} %get-tuple-element.302, ...), kind=kLoop, calls=%fused_computation.6.clone.1 | loop fusion | flops 6881280 | bytes 22282244 | tf_op jit(solution)/shard_map/while/body/eval_jaxpr/add | solution.py:73
  434.4 13.4 %fusion.76 = f32[5,16,16,256]{3,0,2,1:T(8,128)} fusion(f32[5,18,18,256]{3,0,2,1:T(8,128)} %get-tuple-element.300, f32[5,18,18,256]{3,0,2,1:T(8,128)} %copy-done, f32[5,18,18,256]{3,0,2,1:T(8,128)S(1)} %bitcast_convert_fusion.2, f32[5,18,18,256]{3,0,2,1:T(8,128)} %get-tuple-element.301, f32[5,18,18,256]{3,0,2,1:T(8,128)} %get-tuple-element.302, ...), kind=kLoop, calls=%fused_computation.6.clone.1 | loop fusion | flops 6881280 | bytes 22282244 | tf_op jit(solution)/shard_map/while/body/eval_jaxpr/add | solution.py:73
  473.8 13.4 %fusion.76 = f32[5,16,16,256]{3,0,2,1:T(8,128)} fusion(f32[5,18,18,256]{3,0,2,1:T(8,128)} %get-tuple-element.300, f32[5,18,18,256]{3,0,2,1:T(8,128)} %copy-done, f32[5,18,18,256]{3,0,2,1:T(8,128)S(1)} %bitcast_convert_fusion.2, f32[5,18,18,256]{3,0,2,1:T(8,128)} %get-tuple-element.301, f32[5,18,18,256]{3,0,2,1:T(8,128)} %get-tuple-element.302, ...), kind=kLoop, calls=%fused_computation.6.clone.1 | loop fusion | flops 6881280 | bytes 22282244 | tf_op jit(solution)/shard_map/while/body/eval_jaxpr/add | solution.py:73
  513.1 13.4 %fusion.76 = f32[5,16,16,256]{3,0,2,1:T(8,128)} fusion(f32[5,18,18,256]{3,0,2,1:T(8,128)} %get-tuple-element.300, f32[5,18,18,256]{3,0,2,1:T(8,128)} %copy-done, f32[5,18,18,256]{3,0,2,1:T(8,128)S(1)} %bitcast_convert_fusion.2, f32[5,18,18,256]{3,0,2,1:T(8,128)} %get-tuple-element.301, f32[5,18,18,256]{3,0,2,1:T(8,128)} %get-tuple-element.302, ...), kind=kLoop, calls=%fused_computation.6.clone.1 | loop fusion | flops 6881280 | bytes 22282244 | tf_op jit(solution)/shard_map/while/body/eval_jaxpr/add | solution.py:73
  552.5 13.4 %fusion.76 = f32[5,16,16,256]{3,0,2,1:T(8,128)} fusion(f32[5,18,18,256]{3,0,2,1:T(8,128)} %get-tuple-element.300, f32[5,18,18,256]{3,0,2,1:T(8,128)} %copy-done, f32[5,18,18,256]{3,0,2,1:T(8,128)S(1)} %bitcast_convert_fusion.2, f32[5,18,18,256]{3,0,2,1:T(8,128)} %get-tuple-element.301, f32[5,18,18,256]{3,0,2,1:T(8,128)} %get-tuple-element.302, ...), kind=kLoop, calls=%fused_computation.6.clone.1 | loop fusion | flops 6881280 | bytes 22282244 | tf_op jit(solution)/shard_map/while/body/eval_jaxpr/add | solution.py:73
  591.8 13.4 %fusion.76 = f32[5,16,16,256]{3,0,2,1:T(8,128)} fusion(f32[5,18,18,256]{3,0,2,1:T(8,128)} %get-tuple-element.300, f32[5,18,18,256]{3,0,2,1:T(8,128)} %copy-done, f32[5,18,18,256]{3,0,2,1:T(8,128)S(1)} %bitcast_convert_fusion.2, f32[5,18,18,256]{3,0,2,1:T(8,128)} %get-tuple-element.301, f32[5,18,18,256]{3,0,2,1:T(8,128)} %get-tuple-element.302, ...), kind=kLoop, calls=%fused_computation.6.clone.1 | loop fusion | flops 6881280 | bytes 22282244 | tf_op jit(solution)/shard_map/while/body/eval_jaxpr/add | solution.py:73
  631.2 13.4 %fusion.76 = f32[5,16,16,256]{3,0,2,1:T(8,128)} fusion(f32[5,18,18,256]{3,0,2,1:T(8,128)} %get-tuple-element.300, f32[5,18,18,256]{3,0,2,1:T(8,128)} %copy-done, f32[5,18,18,256]{3,0,2,1:T(8,128)S(1)} %bitcast_convert_fusion.2, f32[5,18,18,256]{3,0,2,1:T(8,128)} %get-tuple-element.301, f32[5,18,18,256]{3,0,2,1:T(8,128)} %get-tuple-element.302, ...), kind=kLoop, calls=%fused_computation.6.clone.1 | loop fusion | flops 6881280 | bytes 22282244 | tf_op jit(solution)/shard_map/while/body/eval_jaxpr/add | solution.py:73
  670.6 13.4 %fusion.76 = f32[5,16,16,256]{3,0,2,1:T(8,128)} fusion(f32[5,18,18,256]{3,0,2,1:T(8,128)} %get-tuple-element.300, f32[5,18,18,256]{3,0,2,1:T(8,128)} %copy-done, f32[5,18,18,256]{3,0,2,1:T(8,128)S(1)} %bitcast_convert_fusion.2, f32[5,18,18,256]{3,0,2,1:T(8,128)} %get-tuple-element.301, f32[5,18,18,256]{3,0,2,1:T(8,128)} %get-tuple-element.302, ...), kind=kLoop, calls=%fused_computation.6.clone.1 | loop fusion | flops 6881280 | bytes 22282244 | tf_op jit(solution)/shard_map/while/body/eval_jaxpr/add | solution.py:73
  709.9 13.4 %fusion.76 = f32[5,16,16,256]{3,0,2,1:T(8,128)} fusion(f32[5,18,18,256]{3,0,2,1:T(8,128)} %get-tuple-element.300, f32[5,18,18,256]{3,0,2,1:T(8,128)} %copy-done, f32[5,18,18,256]{3,0,2,1:T(8,128)S(1)} %bitcast_convert_fusion.2, f32[5,18,18,256]{3,0,2,1:T(8,128)} %get-tuple-element.301, f32[5,18,18,256]{3,0,2,1:T(8,128)} %get-tuple-element.302, ...), kind=kLoop, calls=%fused_computation.6.clone.1 | loop fusion | flops 6881280 | bytes 22282244 | tf_op jit(solution)/shard_map/while/body/eval_jaxpr/add | solution.py:73
  749.3 13.4 %fusion.76 = f32[5,16,16,256]{3,0,2,1:T(8,128)} fusion(f32[5,18,18,256]{3,0,2,1:T(8,128)} %get-tuple-element.300, f32[5,18,18,256]{3,0,2,1:T(8,128)} %copy-done, f32[5,18,18,256]{3,0,2,1:T(8,128)S(1)} %bitcast_convert_fusion.2, f32[5,18,18,256]{3,0,2,1:T(8,128)} %get-tuple-element.301, f32[5,18,18,256]{3,0,2,1:T(8,128)} %get-tuple-element.302, ...), kind=kLoop, calls=%fused_computation.6.clone.1 | loop fusion | flops 6881280 | bytes 22282244 | tf_op jit(solution)/shard_map/while/body/eval_jaxpr/add | solution.py:73
  788.6 13.4 %fusion.76 = f32[5,16,16,256]{3,0,2,1:T(8,128)} fusion(f32[5,18,18,256]{3,0,2,1:T(8,128)} %get-tuple-element.300, f32[5,18,18,256]{3,0,2,1:T(8,128)} %copy-done, f32[5,18,18,256]{3,0,2,1:T(8,128)S(1)} %bitcast_convert_fusion.2, f32[5,18,18,256]{3,0,2,1:T(8,128)} %get-tuple-element.301, f32[5,18,18,256]{3,0,2,1:T(8,128)} %get-tuple-element.302, ...), kind=kLoop, calls=%fused_computation.6.clone.1 | loop fusion | flops 6881280 | bytes 22282244 | tf_op jit(solution)/shard_map/while/body/eval_jaxpr/add | solution.py:73
  828.0 13.4 %fusion.76 = f32[5,16,16,256]{3,0,2,1:T(8,128)} fusion(f32[5,18,18,256]{3,0,2,1:T(8,128)} %get-tuple-element.300, f32[5,18,18,256]{3,0,2,1:T(8,128)} %copy-done, f32[5,18,18,256]{3,0,2,1:T(8,128)S(1)} %bitcast_convert_fusion.2, f32[5,18,18,256]{3,0,2,1:T(8,128)} %get-tuple-element.301, f32[5,18,18,256]{3,0,2,1:T(8,128)} %get-tuple-element.302, ...), kind=kLoop, calls=%fused_computation.6.clone.1 | loop fusion | flops 6881280 | bytes 22282244 | tf_op jit(solution)/shard_map/while/body/eval_jaxpr/add | solution.py:73
  862.8 9.6 %collective-permute-start.13 = (f32[5,18,1,256]{3,0,2,1:T(8,128)S(1)}, f32[5,18,1,256]{3,0,2,1:T(8,128)S(1)}, u32[]{:S(2)}, u32[]{:S(2)}) collective-permute-start(f32[5,18,1,256]{3,0,2,1:T(8,128)S(1)} %get-tuple-element.216), channel_id=1, source_target_pairs={{1,0},{2,1},{3,2},{4,3},{5,4},{6,5},{7,6},{8,7},{9,8},{10,9},{11,1... | collective-permute-start | bytes 276488 | tf_op jit(solution)/shard_map/ppermute | solution.py:17
  874.5 9.6 %collective-permute-start.15 = (f32[5,18,1,256]{3,0,2,1:T(8,128)S(1)}, f32[5,18,1,256]{3,0,2,1:T(8,128)S(1)}, u32[]{:S(2)}, u32[]{:S(2)}) collective-permute-start(f32[5,18,1,256]{3,0,2,1:T(8,128)S(1)} %get-tuple-element.214), channel_id=1, source_target_pairs={{1,0},{2,1},{3,2},{4,3},{5,4},{6,5},{7,6},{8,7},{9,8},{10,9},{11,1... | collective-permute-start | bytes 276488 | tf_op jit(solution)/shard_map/ppermute | solution.py:17
  893.8 9.5 %fusion.32 = f32[5,16,16,256]{3,0,2,1:T(8,128)S(1)} fusion(f32[5,18,18,256]{3,0,2,1:T(8,128)} %get-tuple-element.210, f32[5,18,18,256]{3,0,2,1:T(8,128)} %copy-done.10, f32[5,18,18,256]{3,0,2,1:T(8,128)} %get-tuple-element.209, f32[5,18,18,256]{3,0,2,1:T(8,128)} %get-tuple-element.240, f32[5,16,16,1]{3,0,2,1:T(8,128)} %get-tuple-element.228, ...), kind=kLoop, calls=%fused_computation.59 | loop fusion | flops 7536640 | bytes 19124224 | tf_op jit(solution)/shard_map/mul | solution.py:80
  917.6 9.6 %collective-permute-start.19 = (f32[5,18,1,256]{3,0,2,1:T(8,128)S(1)}, f32[5,18,1,256]{3,0,2,1:T(8,128)S(1)}, u32[]{:S(2)}, u32[]{:S(2)}) collective-permute-start(f32[5,18,1,256]{3,0,2,1:T(8,128)S(1)} %get-tuple-element.212), channel_id=1, source_target_pairs={{1,0},{2,1},{3,2},{4,3},{5,4},{6,5},{7,6},{8,7},{9,8},{10,9},{11,1... | collective-permute-start | bytes 276488 | tf_op jit(solution)/shard_map/ppermute | solution.py:17
  937.9 8.6 fusion.26
  (271 shorter events, 479.1 us)
Async XLA Ops:
  0.0 16.0 %copy-start.4 = (f32[5,16,16,256]{3,2,1,0:T(8,128)S(1)}, f32[5,16,16,256]{3,2,1,0:T(8,128)}, u32[]{:S(2)}) copy-start(f32[5,16,16,256]{3,2,1,0:T(8,128)} %param.10) | copy-start | bytes 3932164
  2.3 99.1 %collective-permute-start.6 = (bf16[16,5,1,16,256]{4,3,2,1,0:T(8,128)(2,1)}, bf16[16,5,1,16,256]{4,3,2,1,0:T(8,128)(2,1)}, u32[]{:S(2)}, u32[]{:S(2)}) collective-permute-start(bf16[16,5,1,16,256]{4,3,2,1,0:T(8,128)(2,1)} %get-tuple-element.204), channel_id=1, source_target_pairs={{0,32},{32,64},{64,96},{1,33},{33,65},{65,97},{2,34},{34,66},{66,9... | collective-permute-start | bytes 1966088 | tf_op jit(solution)/shard_map/ppermute | solution.py:15
  4.3 119.2 %collective-permute-start.7 = (bf16[16,5,1,16,256]{4,3,2,1,0:T(8,128)(2,1)S(1)}, bf16[16,5,1,16,256]{4,3,2,1,0:T(8,128)(2,1)}, u32[]{:S(2)}, u32[]{:S(2)}) collective-permute-start(bf16[16,5,1,16,256]{4,3,2,1,0:T(8,128)(2,1)S(1)} %get-tuple-element.203), channel_id=1, source_target_pairs={{32,0},{64,32},{96,64},{33,1},{65,33},{97,65},{34,2},{66,34},{98,6... | collective-permute-start | bytes 1966088 | tf_op jit(solution)/shard_map/ppermute | solution.py:17
  10.4 128.2 %collective-permute-start.2 = (bf16[16,5,1,16,256]{4,3,2,1,0:T(8,128)(2,1)}, bf16[16,5,1,16,256]{4,3,2,1,0:T(8,128)(2,1)}, u32[]{:S(2)}, u32[]{:S(2)}) collective-permute-start(bf16[16,5,1,16,256]{4,3,2,1,0:T(8,128)(2,1)} %get-tuple-element.206), channel_id=1, source_target_pairs={{0,32},{32,64},{64,96},{1,33},{33,65},{65,97},{2,34},{34,66},{66,9... | collective-permute-start | bytes 1966088 | tf_op jit(solution)/shard_map/ppermute | solution.py:15
  12.3 148.0 %collective-permute-start.3 = (bf16[16,5,1,16,256]{4,3,2,1,0:T(8,128)(2,1)}, bf16[16,5,1,16,256]{4,3,2,1,0:T(8,128)(2,1)}, u32[]{:S(2)}, u32[]{:S(2)}) collective-permute-start(bf16[16,5,1,16,256]{4,3,2,1,0:T(8,128)(2,1)} %get-tuple-element.205), channel_id=1, source_target_pairs={{32,0},{64,32},{96,64},{33,1},{65,33},{97,65},{34,2},{66,34},{98,6... | collective-permute-start | bytes 1966088 | tf_op jit(solution)/shard_map/ppermute | solution.py:17
  16.9 79.9 %copy-start.1 = (f32[5,16,16,256]{3,0,2,1:T(8,128)}, f32[5,16,16,256]{3,0,2,1:T(8,128)S(1)}, u32[]{:S(2)}) copy-start(f32[5,16,16,256]{3,0,2,1:T(8,128)S(1)} %copy.42) | copy-start | bytes 3932164
  17.6 80.9 %collective-permute-start.1 = (f32[5,1,16,256]{3,0,2,1:T(8,128)S(1)}, f32[5,1,16,256]{3,0,2,1:T(8,128)S(1)}, u32[]{:S(2)}, u32[]{:S(2)}) collective-permute-start(f32[5,1,16,256]{3,0,2,1:T(8,128)S(1)} %get-tuple-element.232), channel_id=1, source_target_pairs={{0,32},{32,64},{64,96},{1,33},{33,65},{65,97},{2,34},{34,66},{66,9... | collective-permute-start | bytes 245768 | tf_op jit(solution)/shard_map/ppermute | solution.py:15
  98.5 24.9 %copy-start.12 = (f32[5,1,16,256]{3,0,2,1:T(8,128)}, f32[5,1,16,256]{3,0,2,1:T(8,128)S(1)}, u32[]{:S(2)}) copy-start(f32[5,1,16,256]{3,0,2,1:T(8,128)S(1)} %collective-permute-done.1) | copy-start | bytes 245764
  98.5 759.9 %collective-permute-start = (f32[5,1,16,256]{3,0,2,1:T(8,128)}, f32[5,1,16,256]{3,0,2,1:T(8,128)}, u32[]{:S(2)}, u32[]{:S(2)}) collective-permute-start(f32[5,1,16,256]{3,0,2,1:T(8,128)} %get-tuple-element.231), channel_id=1, source_target_pairs={{32,0},{64,32},{96,64},{33,1},{65,33},{97,65},{34,2},{66,34},{98,6... | collective-permute-start | bytes 245768 | tf_op jit(solution)/shard_map/ppermute | solution.py:17
  127.0 48.5 %collective-permute-start.8 = (bf16[16,5,18,1,256]{4,0,3,2,1:T(8,128)(2,1)S(1)}, bf16[16,5,18,1,256]{4,0,3,2,1:T(8,128)(2,1)S(1)}, u32[]{:S(2)}, u32[]{:S(2)}) collective-permute-start(bf16[16,5,18,1,256]{4,0,3,2,1:T(8,128)(2,1)S(1)} %get-tuple-element.199), channel_id=1, source_target_pairs={{0,1},{1,2},{2,3},{3,4},{4,5},{5,6},{6,7},{7,8},{8,9},{9,10},{10,1... | collective-permute-start | bytes 2211848 | tf_op jit(solution)/shard_map/ppermute | solution.py:15
  130.2 45.4 %collective-permute-start.9 = (bf16[16,5,18,1,256]{4,0,3,2,1:T(8,128)(2,1)S(1)}, bf16[16,5,18,1,256]{4,0,3,2,1:T(8,128)(2,1)S(1)}, u32[]{:S(2)}, u32[]{:S(2)}) collective-permute-start(bf16[16,5,18,1,256]{4,0,3,2,1:T(8,128)(2,1)S(1)} %get-tuple-element.200), channel_id=1, source_target_pairs={{1,0},{2,1},{3,2},{4,3},{5,4},{6,5},{7,6},{8,7},{9,8},{10,9},{11,1... | collective-permute-start | bytes 2211848 | tf_op jit(solution)/shard_map/ppermute | solution.py:17
  163.9 33.0 %collective-permute-start.4 = (bf16[16,5,18,1,256]{4,0,3,2,1:T(8,128)(2,1)S(1)}, bf16[16,5,18,1,256]{4,0,3,2,1:T(8,128)(2,1)S(1)}, u32[]{:S(2)}, u32[]{:S(2)}) collective-permute-start(bf16[16,5,18,1,256]{4,0,3,2,1:T(8,128)(2,1)S(1)} %get-tuple-element.201), channel_id=1, source_target_pairs={{0,1},{1,2},{2,3},{3,4},{4,5},{5,6},{6,7},{7,8},{8,9},{9,10},{10,1... | collective-permute-start | bytes 2211848 | tf_op jit(solution)/shard_map/ppermute | solution.py:15
  165.9 31.1 %collective-permute-start.5 = (bf16[16,5,18,1,256]{4,0,3,2,1:T(8,128)(2,1)S(1)}, bf16[16,5,18,1,256]{4,0,3,2,1:T(8,128)(2,1)S(1)}, u32[]{:S(2)}, u32[]{:S(2)}) collective-permute-start(bf16[16,5,18,1,256]{4,0,3,2,1:T(8,128)(2,1)S(1)} %get-tuple-element.202), channel_id=1, source_target_pairs={{1,0},{2,1},{3,2},{4,3},{5,4},{6,5},{7,6},{8,7},{9,8},{10,9},{11,1... | collective-permute-start | bytes 2211848 | tf_op jit(solution)/shard_map/ppermute | solution.py:17
  175.5 21.4 %slice-start = ((s8[11796480]{0:T(1024)(128)(4,1)}), s8[4194304]{0:T(1024)(128)(4,1)S(1)}, s32[]{:S(2)}) async-start(s8[11796480]{0:T(1024)(128)(4,1)} %bitcast.119), calls=%async_computation | async-start | bytes 8388608
  175.5 21.4 %slice-start.1 = ((s8[11796480]{0:T(1024)(128)(4,1)}), s8[4194304]{0:T(1024)(128)(4,1)S(1)}, s32[]{:S(2)}) async-start(s8[11796480]{0:T(1024)(128)(4,1)} %bitcast.119), calls=%async_computation.1 | async-start | bytes 8388608
  183.3 13.6 %slice-start.2 = ((s8[11796480]{0:T(1024)(128)(4,1)}), s8[3407872]{0:T(1024)(128)(4,1)S(1)}, s32[]{:S(2)}) async-start(s8[11796480]{0:T(1024)(128)(4,1)} %bitcast.119), calls=%async_computation.2 | async-start | bytes 6815744
  198.7 13.6 %copy-start.17 = (s32[16]{0:T(128)S(1)}, s32[16]{0:T(128)}, u32[]{:S(2)}) copy-start(s32[16]{0:T(128)} %param.12) | copy-start | bytes 196
  212.3 629.4 %copy-start.14 = (f32[16,16,256]{2,1,0:T(8,128)S(1)}, f32[16,16,256]{2,1,0:T(8,128)}, u32[]{:S(2)}) copy-start(f32[16,16,256]{2,1,0:T(8,128)} %get-tuple-element.238) | copy-start | bytes 786436
  229.9 7.6 copy-start
  268.7 7.6 copy-start
  308.0 7.6 copy-start
  347.4 7.6 copy-start
  852.8 6.5 collective-permute-start.10
  854.7 6.1 collective-permute-start.11
  860.9 23.2 %collective-permute-start.12 = (f32[5,18,1,256]{3,0,2,1:T(8,128)S(1)}, f32[5,18,1,256]{3,0,2,1:T(8,128)S(1)}, u32[]{:S(2)}, u32[]{:S(2)}) collective-permute-start(f32[5,18,1,256]{3,0,2,1:T(8,128)S(1)} %get-tuple-element.215), channel_id=1, source_target_pairs={{0,1},{1,2},{2,3},{3,4},{4,5},{5,6},{6,7},{7,8},{8,9},{9,10},{10,1... | collective-permute-start | bytes 276488 | tf_op jit(solution)/shard_map/ppermute | solution.py:15
  862.8 21.3 %collective-permute-start.13 = (f32[5,18,1,256]{3,0,2,1:T(8,128)S(1)}, f32[5,18,1,256]{3,0,2,1:T(8,128)S(1)}, u32[]{:S(2)}, u32[]{:S(2)}) collective-permute-start(f32[5,18,1,256]{3,0,2,1:T(8,128)S(1)} %get-tuple-element.216), channel_id=1, source_target_pairs={{1,0},{2,1},{3,2},{4,3},{5,4},{6,5},{7,6},{8,7},{9,8},{10,9},{11,1... | collective-permute-start | bytes 276488 | tf_op jit(solution)/shard_map/ppermute | solution.py:17
  872.5 14.2 %collective-permute-start.14 = (f32[5,18,1,256]{3,0,2,1:T(8,128)S(1)}, f32[5,18,1,256]{3,0,2,1:T(8,128)S(1)}, u32[]{:S(2)}, u32[]{:S(2)}) collective-permute-start(f32[5,18,1,256]{3,0,2,1:T(8,128)S(1)} %get-tuple-element.213), channel_id=1, source_target_pairs={{0,1},{1,2},{2,3},{3,4},{4,5},{5,6},{6,7},{7,8},{8,9},{9,10},{10,1... | collective-permute-start | bytes 276488 | tf_op jit(solution)/shard_map/ppermute | solution.py:15
  874.5 12.3 %collective-permute-start.15 = (f32[5,18,1,256]{3,0,2,1:T(8,128)S(1)}, f32[5,18,1,256]{3,0,2,1:T(8,128)S(1)}, u32[]{:S(2)}, u32[]{:S(2)}) collective-permute-start(f32[5,18,1,256]{3,0,2,1:T(8,128)S(1)} %get-tuple-element.214), channel_id=1, source_target_pairs={{1,0},{2,1},{3,2},{4,3},{5,4},{6,5},{7,6},{8,7},{9,8},{10,9},{11,1... | collective-permute-start | bytes 276488 | tf_op jit(solution)/shard_map/ppermute | solution.py:17
  907.4 8.2 collective-permute-start.16
  909.3 6.3 collective-permute-start.17
  915.7 12.8 %collective-permute-start.18 = (f32[5,18,1,256]{3,0,2,1:T(8,128)S(1)}, f32[5,18,1,256]{3,0,2,1:T(8,128)S(1)}, u32[]{:S(2)}, u32[]{:S(2)}) collective-permute-start(f32[5,18,1,256]{3,0,2,1:T(8,128)S(1)} %get-tuple-element.211), channel_id=1, source_target_pairs={{0,1},{1,2},{2,3},{3,4},{4,5},{5,6},{6,7},{7,8},{8,9},{9,10},{10,1... | collective-permute-start | bytes 276488 | tf_op jit(solution)/shard_map/ppermute | solution.py:15
  917.6 12.3 %collective-permute-start.19 = (f32[5,18,1,256]{3,0,2,1:T(8,128)S(1)}, f32[5,18,1,256]{3,0,2,1:T(8,128)S(1)}, u32[]{:S(2)}, u32[]{:S(2)}) collective-permute-start(f32[5,18,1,256]{3,0,2,1:T(8,128)S(1)} %get-tuple-element.212), channel_id=1, source_target_pairs={{1,0},{2,1},{3,2},{4,3},{5,4},{6,5},{7,6},{8,7},{9,8},{10,9},{11,1... | collective-permute-start | bytes 276488 | tf_op jit(solution)/shard_map/ppermute | solution.py:17
  (24 other events, 151.2 us)
where the time goes:
time: 959 us; the launch traced here: 948 us
  other arithmetic  277 us (29%)
  matrix products  247 us (26%)
  local copies, waits for them, and re-layouts  236 us (25%)
  starting transfers between devices  84.2 us (9%)
  blocking collectives  67.5 us (7%)
  loops' own time  32 us (3%)
    dot_general x54, matrix products, mixing(): jnp.einsum('ij,i...->j...', matrix, field_in, precision=lax.Precision.HIG...  247 us
    add x16, other arithmetic, accumulate(): return summed + amplitude[number] * bilinear_term(direct, adjoint, flux_mix)  214 us
    slice x38, local copies, waits for them, and re-layouts, diff_span(): return jnp.roll(field_in, -1, -1) - jnp.roll(field_in, 1, -1)  127 us
    unnamed x49, local copies, waits for them, and re-layouts  74.3 us
    psum x1, blocking collectives, per_device(): energy = lax.psum(local_sums, ('chord', 'normal')) / cells_all  67.5 us
    ppermute x10, starting transfers between devices, with_halo(): lax.ppermute(head, axis, [((i + 1) % count, i) for i in range(ends)])  63.8 us
    another operation x1, loops' own time, per_device(): lax.fori_loop(0, modes_count, accumulate, zeros_field) / modes_count  32 us
    convert_element_type x16, other arithmetic, accumulate(): direct = direct_pad[number].astype(jnp.float32)  25.6 us
  transfers between devices with their start and end apart: 20, of which 4 were waited for; matrix products, arithmetic and copies ran while one was open for 76% of the time, Pallas kernels for 0%

commit v1 on v0

v1 whole, which is shorter than its diff:
```python
import functools

import jax
import jax.numpy as jnp
from jax import lax
from jax.experimental import pallas as pl
from jax.experimental.pallas import tpu as pltpu
from jax.sharding import PartitionSpec as P

MESH = pl.DeviceIdType.MESH
F32 = jnp.float32
BF16 = jnp.bfloat16
GROUP = 4


def iota(shape, dim):
    return lax.broadcasted_iota(jnp.int32, shape, dim)


def diff_lanes(x):
    lanes = x.shape[-1]
    return pltpu.roll(x, lanes - 1, 1) - pltpu.roll(x, 1, 1)


def rows_up(x):
    rows = x.shape[0]
    return jnp.where(iota(x.shape, 0) == rows - 1, 0.0, pltpu.roll(x, rows - 1, 0))


def rows_down(x):
    return jnp.where(iota(x.shape, 0) == 0, 0.0, pltpu.roll(x, 1, 0))


def split3(x):
    high = x.astype(BF16)
    low = (x - high.astype(F32)).astype(BF16)
    return jnp.concatenate([high, low, high], axis=0)


def dot(a, b):
    return jnp.dot(a, b, preferred_element_type=F32)


def kernel(
    sizes,
    u_hbm, v_hbm, base_hbm, cell_hbm, pick, mix,
    out_hbm,
    u, v, base, cell, uface, vface, uhalo, wface, mats, mat2, mat0, select, circ,
    w_scr, du_scr, acc, grad, sx, sface, shalo, ysend, yhalo, field, wall, base_dz, bface, bhalo,
    fterm, energy, round_one, round_two, round_three, amp, weight, result,
    load_sem, usend_sem, urecv_sem, xs_sem, xr_sem, ys_sem, yr_sem, es_sem, er_sem, out_sem,
):
    nc, nn, modes, nv, nx, ny, nz = sizes
    kv = nv * ny
    c, n = lax.axis_index("chord"), lax.axis_index("normal")
    has_x = (c > 0, c < nc - 1)
    has_y = (n > 0, n < nn - 1)
    step = (-1, 1)
    zs, rest = 4, nn // 4
    groups = modes // GROUP

    def u_load(g):
        s = pl.ds(g * GROUP, GROUP)
        return pltpu.make_async_copy(u_hbm.at[s], u.at[s, :, pl.ds(1, nx)], load_sem.at[g])

    def v_load(g):
        s = pl.ds(g * GROUP, GROUP)
        return pltpu.make_async_copy(v_hbm.at[s], v.at[s], load_sem.at[groups + g])

    base_load = pltpu.make_async_copy(base_hbm, base.at[:, pl.ds(1, nx)], load_sem.at[2 * groups])
    cell_load = pltpu.make_async_copy(cell_hbm, cell, load_sem.at[2 * groups + 1])
    for g in range(groups):
        u_load(g).start()
    base_load.start()
    cell_load.start()
    for g in range(groups):
        v_load(g).start()

    first = [(lax.rem(c + k, nc), n) for k in range(1, nc)]
    second = [(c, n // zs * zs + lax.rem(lax.rem(n, zs) + k, zs)) for k in range(1, zs)]
    third = [(c, lax.rem(n // zs + k, rest) * zs + lax.rem(n, zs)) for k in range(1, rest)]
    around = [(c, lax.rem(n + 1, nn)), (c, lax.rem(n + nn - 1, nn))]
    barrier = pltpu.get_barrier_semaphore()
    peers = first + second + third + around
    for peer in peers:
        pl.semaphore_signal(barrier, inc=1, device_id=peer, device_id_type=MESH)

    @pl.when(c == 0)
    def _():
        u[:, :, 0] = jnp.zeros((modes, nv, ny, nz), BF16)
        base[:, 0] = jnp.zeros((nv, ny, nz), F32)
        sx[:, 0] = jnp.zeros((nv, ny, nz), F32)
        field[0, :, 0] = jnp.zeros((nv, ny, nz), F32)
        field[1, :, 0] = jnp.zeros((nv, ny, nz), F32)

    @pl.when(c == nc - 1)
    def _():
        u[:, :, nx + 1] = jnp.zeros((modes, nv, ny, nz), BF16)
        base[:, nx + 1] = jnp.zeros((nv, ny, nz), F32)
        sx[:, nx + 1] = jnp.zeros((nv, ny, nz), F32)
        field[0, :, nx + 1] = jnp.zeros((nv, ny, nz), F32)
        field[1, :, nx + 1] = jnp.zeros((nv, ny, nz), F32)

    for side, at_edge in ((0, n == 0), (1, n == nn - 1)):
        @pl.when(at_edge)
        def _():
            uhalo[side] = jnp.zeros((modes, nv, nx, nz), BF16)
            bhalo[side] = jnp.zeros((nv, nx, nz), F32)
            shalo[side] = jnp.zeros((nv, nx, nz), F32)
            yhalo[0, side] = jnp.zeros((nv, nx, nz), F32)
            yhalo[1, side] = jnp.zeros((nv, nx, nz), F32)

    pl.semaphore_wait(barrier, len(peers))

    def x_copy(kind, way, src, dst):
        return pltpu.make_async_remote_copy(
            src_ref=src, dst_ref=dst, send_sem=xs_sem.at[kind, way], recv_sem=xr_sem.at[kind, 1 - way],
            device_id=(lax.rem(c + step[way] + nc, nc), n), device_id_type=MESH)

    def y_copy(send_sems, recv_sems, kind, way, src, dst):
        return pltpu.make_async_remote_copy(
            src_ref=src, dst_ref=dst, send_sem=send_sems.at[kind, way], recv_sem=recv_sems.at[kind, 1 - way],
            device_id=(c, lax.rem(n + step[way] + nn, nn)), device_id_type=MESH)

    x_links = [
        lambda w: x_copy(0, w, u_hbm.at[:, :, (nx - 1) * w], u.at[:, :, (nx + 1) * (1 - w)]),
        lambda w: x_copy(1, w, base_hbm.at[:, (nx - 1) * w], base.at[:, (nx + 1) * (1 - w)]),
        lambda w: x_copy(2, w, sx.at[:, 1 + (nx - 1) * w], sx.at[:, (nx + 1) * (1 - w)]),
        lambda w: x_copy(3, w, field.at[0, :, 1 + (nx - 1) * w], field.at[0, :, (nx + 1) * (1 - w)]),
        lambda w: x_copy(4, w, field.at[1, :, 1 + (nx - 1) * w], field.at[1, :, (nx + 1) * (1 - w)]),
    ]
    y_links = [
        lambda w: y_copy(ys_sem, yr_sem, 0, w, bface.at[w], bhalo.at[1 - w]),
        lambda w: y_copy(ys_sem, yr_sem, 1, w, sface.at[w], shalo.at[1 - w]),
        lambda w: y_copy(ys_sem, yr_sem, 2, w, ysend.at[0, w], yhalo.at[0, 1 - w]),
        lambda w: y_copy(ys_sem, yr_sem, 3, w, ysend.at[1, w], yhalo.at[1, 1 - w]),
    ]

    def u_link(g):
        s = pl.ds(g * GROUP, GROUP)
        return lambda w: y_copy(usend_sem, urecv_sem, g, w, uface.at[w, s], uhalo.at[1 - w, s])

    def send(link, has):
        for w in (0, 1):
            @pl.when(has[w])
            def _():
                link(w).start()

    def receive(link, has):
        for side in (0, 1):
            @pl.when(has[side])
            def _():
                link(1 - side).wait_recv()

    def drain(link, has):
        for w in (0, 1):
            @pl.when(has[w])
            def _():
                link(w).wait_send()

    send(x_links[0], has_x)
    send(x_links[1], has_x)

    pick_row = iota((2 * nx, nx * ny), 0)
    from_row = iota((2 * nx, nx * ny), 1)
    wanted = jnp.where(pick_row < nx, pick_row * ny, (pick_row - nx) * ny + ny - 1)
    select[...] = jnp.where(from_row == wanted, 1.0, 0.0).astype(BF16)
    lane_in, lane_out = iota((nz, nz), 0), iota((nz, nz), 1)
    ahead = jnp.where(lane_out == nz - 1, 0, lane_out + 1)
    behind = jnp.where(lane_out == 0, nz - 1, lane_out - 1)
    circ[...] = (jnp.where(lane_in == ahead, 1.0, 0.0) - jnp.where(lane_in == behind, 1.0, 0.0)).astype(BF16)

    def faces_of(block, faces, m):
        for i in range(nv):
            both = dot(select[...], block(m, i).reshape(nx * ny, nz))
            faces[0, m, i] = both[:nx].astype(BF16)
            faces[1, m, i] = both[nx:].astype(BF16)

    for g in range(groups):
        u_load(g).wait()

        def u_mode(m, carry):
            total = jnp.zeros((ny, nz), F32)
            for i in range(nv):
                for x in range(nx):
                    cells = u[m, i, 1 + x].astype(F32)
                    total = total + cells * cells
            total = jnp.sum(total, axis=0, keepdims=True)
            energy[pl.ds(m, 1), :] = total[:, :128] + total[:, 128:]
            faces_of(lambda m, i: u[m, i, pl.ds(1, nx)], uface, m)
            return carry

        lax.fori_loop(g * GROUP, (g + 1) * GROUP, u_mode, 0)
        send(u_link(g), has_y)

    def e_copy(index, peer, dst):
        return pltpu.make_async_remote_copy(
            src_ref=energy.at[pl.ds(modes * (0 if index < nc - 1 else 1 if index < nc + zs - 2 else 2), modes)],
            dst_ref=dst, send_sem=es_sem.at[index], recv_sem=er_sem.at[index], device_id=peer, device_id_type=MESH)

    ones = [e_copy(k, first[k], round_one.at[k]) for k in range(nc - 1)]
    twos = [e_copy(nc - 1 + k, second[k], round_two.at[k]) for k in range(zs - 1)]
    threes = [e_copy(nc + zs - 2 + k, third[k], round_three.at[k]) for k in range(rest - 1)]

    def v_faces(g):
        v_load(g).wait()

        def v_mode(m, carry):
            faces_of(lambda m, i: v[m, i], vface, m)
            return carry

        lax.fori_loop(g * GROUP, (g + 1) * GROUP, v_mode, 0)

    def finish(copies, slots, src):
        total = energy[pl.ds(modes * src, modes), :]
        for k, copy in enumerate(copies):
            copy.wait_recv()
            total = total + slots[k]
        return total

    for copy in ones:
        copy.start()
    v_faces(0)
    energy[pl.ds(modes, modes), :] = finish(ones, round_one, 0)
    for copy in twos:
        copy.start()

    width = 3 * kv
    lane = iota((ny, width), 1)
    row = iota((ny, width), 0)
    lane_row = lax.rem(lane, ny)
    lane_var = lax.rem(lane, kv) // ny
    same = jnp.where(lane_row == row, 1.0, 0.0)
    nxt = jnp.where(lane_row == row + 1, 1.0, 0.0)
    prv = jnp.where(lane_row == row - 1, 1.0, 0.0)
    kinds = ((0, same), (1, nxt - same), (1, same - prv), (2, same), (1, same))
    for k, (d, stencil) in enumerate(kinds):
        for j in range(nv):
            coefs = jnp.zeros((ny, width), F32)
            for i in range(nv):
                coefs = jnp.where(lane_var == i, mix[d, i, j], coefs)
            mat0[pl.ds((k * nv + j) * ny, ny), :] = coefs * stencil
    high = mat0[...].astype(BF16)
    low = (mat0[...] - high.astype(F32)).astype(BF16)
    mat2[...] = jnp.where(iota(mat0.shape, 1) < 2 * kv, high.astype(F32), low.astype(F32)).astype(BF16)

    v_faces(1)
    energy[pl.ds(2 * modes, modes), :] = finish(twos, round_two, 1)
    for copy in threes:
        copy.start()
    v_faces(2)

    cell_load.wait()
    base_load.wait()
    kind_of = cell[...]
    weight[...] = jnp.where(kind_of == 0, 1.0, jnp.where(kind_of == 1, 0.5, 0.0)).astype(F32)
    for side in (0, 1):
        for x in range(nx):
            bface[side, :, pl.ds(x, 1), :] = base[:, 1 + x, pl.ds((ny - 1) * side, 1), :]
    send(y_links[0], has_y)

    def base_plane(x, carry):
        for j in range(nv):
            base_dz[j, x] = diff_lanes(base[j, 1 + x])
        return carry

    lax.fori_loop(0, nx, base_plane, 0)
    v_faces(3)

    cells_all = nc * nn * nv * nx * ny * nz
    total = jnp.sum(finish(threes, round_three, 2), axis=1, keepdims=True)
    amp[...] = jnp.broadcast_to(lax.rsqrt(total / cells_all + 1e-06) / modes, amp.shape)

    def mode_matrix(m, carry):
        scaled = mat0[:, pl.ds(0, 2 * kv)] * amp[pl.ds(m, 1), pl.ds(0, 2 * kv)]
        big = scaled.astype(BF16).astype(F32)
        mats[m] = jnp.where(iota(scaled.shape, 1) < kv, big, scaled - big).astype(BF16)
        return carry

    lax.fori_loop(0, modes, mode_matrix, 0)

    sface[...] = jnp.zeros(sface.shape, F32)
    sx[:, 1] = jnp.zeros((nv, ny, nz), F32)
    sx[:, nx] = jnp.zeros((nv, ny, nz), F32)

    def face_mode(m, carry):
        p = pick[m]
        for s in (0, 1):
            rows = vface[s, p].reshape(kv, nz)
            w = dot(mats[m, pl.ds(4 * kv, kv), :], jnp.concatenate([rows, rows], axis=0))
            wface[s, m] = w
            sface[s] += w.reshape(nv, nx, nz) * uface[s, m].astype(F32)
            rows = v[p, :, (nx - 1) * s].reshape(kv, nz)
            w = dot(mats[m, pl.ds(0, kv), :], jnp.concatenate([rows, rows], axis=0))
            x = 1 + (nx - 1) * s
            sx[:, x] += w.reshape(nv, ny, nz) * u[m, :, x].astype(F32)
        return carry

    lax.fori_loop(0, modes, face_mode, 0)
    send(x_links[2], has_x)
    send(y_links[1], has_y)

    def plane(x):
        def group(g, carry):
            m0 = g * GROUP
            du_scr[...] = dot(u[pl.ds(m0, GROUP), :, x].reshape(GROUP * kv, nz), circ[...])
            for k in range(GROUP):
                rows = v[pick[m0 + k], :, x - 1].reshape(kv, nz)
                w_scr[k] = dot(mats[m0 + k, pl.ds(0, 4 * kv), :], jnp.concatenate([rows, rows], axis=0))
            for j in range(nv):
                q, s_x, s_z, up, down = (acc[t, j] for t in range(5))
                for k in range(GROUP):
                    here = u[m0 + k, j, x].astype(F32)
                    dx = u[m0 + k, j, x + 1].astype(F32) - u[m0 + k, j, x - 1].astype(F32)
                    dz = du_scr[pl.ds(k * kv + j * ny, ny), :]
                    wx, wp, wm, wz = (w_scr[k, pl.ds(t * kv + j * ny, ny), :] for t in range(4))
                    q = q + dx * wx + dz * wz
                    s_x = s_x + here * wx
                    s_z = s_z + here * wz
                    up = up + here * wm
                    down = down + here * wp
                for t, value in enumerate((q, s_x, s_z, up, down)):
                    acc[t, j] = value
            return carry

        acc[...] = jnp.zeros(acc.shape, F32)
        lax.fori_loop(0, groups, group, 0)
        for j in range(nv):
            grad[j, x - 1] = acc[0, j] - diff_lanes(acc[2, j]) - rows_up(acc[3, j]) - rows_down(acc[4, j])

    def inner_plane(x, carry):
        plane(x)
        for j in range(nv):
            sx[j, x] = acc[1, j]
        return carry

    lax.fori_loop(2, nx, inner_plane, 0)
    receive(x_links[0], has_x)

    def end_plane(s, carry):
        plane(1 + (nx - 1) * s)
        return carry

    lax.fori_loop(0, 2, end_plane, 0)

    for g in range(groups):
        receive(u_link(g), has_y)
    fterm[...] = jnp.zeros(fterm.shape, F32)

    def cross_mode(m, carry):
        for s in (0, 1):
            fterm[s] += wface[s, m].reshape(nv, nx, nz) * uhalo[s, m].astype(F32)
        return carry

    lax.fori_loop(0, modes, cross_mode, 0)
    receive(y_links[1], has_y)
    receive(x_links[2], has_x)
    fterm[0] = shalo[0] - fterm[0]
    fterm[1] = fterm[1] - shalo[1]

    def add_rows(target, x0):
        for side in (0, 1):
            for x in range(nx):
                end = pl.ds((ny - 1) * side, 1)
                target[:, x + x0, end, :] = target[:, x + x0, end, :] + fterm[side, :, pl.ds(x, 1), :]

    def grad_plane(x, carry):
        for j in range(nv):
            grad[j, x] = grad[j, x] - (sx[j, x + 2] - sx[j, x])
        return carry

    lax.fori_loop(0, nx, grad_plane, 0)
    add_rows(grad, 0)

    def apply(slot, source, target):
        def weigh(x, carry):
            for j in range(nv):
                field[slot, j, x + 1] = weight[x] * source[j, x]
            return carry

        lax.fori_loop(0, nx, weigh, 0)
        for side in (0, 1):
            for x in range(nx):
                ysend[slot, side, :, pl.ds(x, 1), :] = field[slot, :, 1 + x, pl.ds((ny - 1) * side, 1), :]
        send(x_links[3 + slot], has_x)
        send(y_links[2 + slot], has_y)

        def mixed(x, carry):
            wall[x] = dot(mat2[pl.ds(0, 4 * kv), :], split3(field[slot, :, x].reshape(kv, nz)))
            return carry

        lax.fori_loop(1, nx + 1, mixed, 0)
        own = [dot(mat2[pl.ds(4 * kv, kv), :], split3(ysend[slot, s].reshape(kv, nz))) for s in (0, 1)]
        for s in (0, 1):
            wface[s, 0] = own[s]

        def result_plane(x, carry):
            for j in range(nv):
                r = pl.ds(j * ny, ny)
                wx = wall[x, r, :]
                wp, wm, wz = (wall[x, pl.ds(t * kv + j * ny, ny), :] for t in (1, 2, 3))
                here = base[j, x]
                value = base[j, x + 1] * (wx - wall[x + 1, r, :]) - base[j, x - 1] * (wx - wall[x - 1, r, :])
                value = value + base_dz[j, x - 1] * wz - diff_lanes(here * wz)
                target[j, x - 1] = value - rows_up(here * wm) - rows_down(here * wp)
            return carry

        lax.fori_loop(2, nx, result_plane, 0)
        if slot == 0:
            receive(x_links[1], has_x)
            receive(y_links[0], has_y)
        receive(x_links[3 + slot], has_x)
        receive(y_links[2 + slot], has_y)
        for x in (0, nx + 1):
            wall[x, pl.ds(0, kv), :] = dot(mat2[pl.ds(0, kv), :], split3(field[slot, :, x].reshape(kv, nz)))
        lax.fori_loop(0, 2, lambda s, carry: result_plane(1 + (nx - 1) * s, carry), 0)
        for s in (0, 1):
            far = dot(mat2[pl.ds(4 * kv, kv), :], split3(yhalo[slot, s].reshape(kv, nz)))
            change = (far - wface[s, 0]).reshape(nv, nx, nz) * bhalo[s]
            fterm[s] = change if s == 0 else -change
        add_rows(target, 0)

    apply(0, grad, result)
    apply(1, result, grad)
    store = pltpu.make_async_copy(grad, out_hbm, out_sem)
    store.start()
    for g in range(groups):
        drain(u_link(g), has_y)
    for link in x_links:
        drain(link, has_x)
    for link in y_links:
        drain(link, has_y)
    for copy in ones + twos + threes:
        copy.wait_send()
    store.wait()


def per_device(u, v, base, cell, pick, mix, *, interpret=False):
    modes, nv, nx, ny, nz = u.shape
    nc, nn = lax.axis_size("chord"), lax.axis_size("normal")
    kv = nv * ny
    groups = modes // GROUP
    vm = pltpu.VMEM
    any_space = pl.BlockSpec(memory_space=pl.ANY)
    smem = pl.BlockSpec(memory_space=pltpu.SMEM)
    return pl.pallas_call(
        functools.partial(kernel, (nc, nn, modes, nv, nx, ny, nz)),
        out_shape=jax.ShapeDtypeStruct(base.shape, F32),
        in_specs=[any_space] * 4 + [smem] * 2,
        out_specs=any_space,
        scratch_shapes=[
            vm((modes, nv, nx + 2, ny, nz), BF16),
            vm((modes, nv, nx, ny, nz), BF16),
            vm((nv, nx + 2, ny, nz), F32),
            vm((nx, ny, nz), jnp.int32),
            vm((2, modes, nv, nx, nz), BF16),
            vm((2, modes, nv, nx, nz), BF16),
            vm((2, modes, nv, nx, nz), BF16),
            vm((2, modes, kv, nz), F32),
            vm((modes, 5 * kv, 2 * kv), BF16),
            vm((5 * kv, 3 * kv), BF16),
            vm((5 * kv, 3 * kv), F32),
            vm((2 * nx, nx * ny), BF16),
            vm((nz, nz), BF16),
            vm((GROUP, 4 * kv, nz), F32),
            vm((GROUP * kv, nz), F32),
            vm((5, nv, ny, nz), F32),
            vm((nv, nx, ny, nz), F32),
            vm((nv, nx + 2, ny, nz), F32),
            vm((2, nv, nx, nz), F32),
            vm((2, nv, nx, nz), F32),
            vm((2, 2, nv, nx, nz), F32),
            vm((2, 2, nv, nx, nz), F32),
            vm((2, nv, nx + 2, ny, nz), F32),
            vm((nx + 2, 4 * kv, nz), F32),
            vm((nv, nx, ny, nz), F32),
            vm((2, nv, nx, nz), F32),
            vm((2, nv, nx, nz), F32),
            vm((2, nv, nx, nz), F32),
            vm((3 * modes, 128), F32),
            vm((nc - 1, modes, 128), F32),
            vm((3, modes, 128), F32),
            vm((max(nn // 4 - 1, 1), modes, 128), F32),
            vm((modes, 256), F32),
            vm((nx, ny, nz), F32),
            vm((nv, nx, ny, nz), F32),
            pltpu.SemaphoreType.DMA((2 * groups + 2,)),
            pltpu.SemaphoreType.DMA((groups, 2)),
            pltpu.SemaphoreType.DMA((groups, 2)),
            pltpu.SemaphoreType.DMA((5, 2)),
            pltpu.SemaphoreType.DMA((5, 2)),
            pltpu.SemaphoreType.DMA((4, 2)),
            pltpu.SemaphoreType.DMA((4, 2)),
            pltpu.SemaphoreType.DMA((nc + nn // 4 + 1,)),
            pltpu.SemaphoreType.DMA((nc + nn // 4 + 1,)),
            pltpu.SemaphoreType.DMA,
        ],
        compiler_params=pltpu.CompilerParams(
            collective_id=0, has_side_effects=True, vmem_limit_bytes=60 * 2**20),
    )(u, v, base, cell, pick, mix)


def solution(mesh):
    return jax.shard_map(
        per_device,
        mesh=mesh,
        in_specs=(
            P(None, None, "chord", "normal", None),
            P(None, None, "chord", "normal", None),
            P(None, "chord", "normal", None),
            P("chord", "normal", None),
            P(),
            P(),
        ),
        out_specs=P(None, "chord", "normal", None),
        check_vma=False,
    )
```

time: 959 us -> 97.6 us (0.10); the launches traced: 948 us -> 97.4 us
  other arithmetic: 277 us -> 0 us
  matrix products: 247 us -> 0 us
  local copies, waits for them, and re-layouts: 236 us -> 3.82 us
  Pallas kernels: 0 us -> 93.5 us
  starting transfers between devices: 84.2 us -> 0 us
  blocking collectives: 67.5 us -> 0 us
  loops' own time: 32 us -> 0 us
    dot_general x54 -> x0, matrix products: 247 us -> none  [mixing(): jnp.einsum('ij,i...->j...', matrix, field_in, precision=lax.Precision.HIG...]
    add x16 -> x0, other arithmetic: 214 us -> none  [accumulate(): return summed + amplitude[number] * bilinear_term(direct, adjoint, flux_mix)]
    slice x46 -> x0, local copies, waits for them, and re-layouts: 135 us -> none  [the longest x38 127 us: diff_span(): return jnp.roll(field_in, -1, -1) - jnp.roll(field_in, 1, -1)]
    pallas_call x0 -> x1, Pallas kernels: none -> 93.5 us  [per_device(): pl.pallas_call(functools.partial(kernel, (nc, nn, modes, nv, nx, ny, nz))...]
    ppermute x20 -> x0, starting transfers between devices: 84.2 us -> none  [the longest x10 63.8 us: with_halo(): lax.ppermute(head, axis, [((i + 1) % count, i) for i in range(ends)])]
    unnamed x49 -> x2, local copies, waits for them, and re-layouts: 74.3 us -> 3.82 us
    psum x1 -> x0, blocking collectives: 67.5 us -> none  [per_device(): energy = lax.psum(local_sums, ('chord', 'normal')) / cells_all]
    another operation x1 -> x0, loops' own time: 32 us -> none  [per_device(): lax.fori_loop(0, modes_count, accumulate, zeros_field) / modes_count]
  transfers between devices with their start and end apart: 20 -> 0, of which waited for: 4 -> 0; matrix products, arithmetic and copies ran while one was open for 76% -> 0% of each run, Pallas kernels for 0% -> 0%
where the time goes in v1:
time: 97.6 us; the launch traced here: 97.4 us
  Pallas kernels  93.5 us (96%)
  local copies, waits for them, and re-layouts  3.82 us (4%)
    pallas_call x1, Pallas kernels, per_device(): pl.pallas_call(functools.partial(kernel, (nc, nn, modes, nv, nx, ny, nz))...  93.5 us
    unnamed x2, local copies, waits for them, and re-layouts  3.82 us

profile of v1, /device:TPU:6, one launch (start us, length us, event | category | flops | bytes accessed | tf_op | source)
XLA Modules:
  0.0 97.4 jit_solution(3445156319465451346)
XLA Ops:
  0.0 1.3 %copy.7.mix = f32[3,5,5]{2,1,0:T(8,128)} copy(f32[3,5,5]{2,0,1:T(4,128)} %param.11) | data formatting | bytes 600 | tf_op args[5]
  1.3 93.5 %shard_map.64 = f32[5,16,16,256]{3,2,1,0:T(8,128)} custom-call(bf16[16,5,16,16,256]{4,3,2,1,0:T(8,128)(2,1)} %u_hbm.1, bf16[16,5,16,16,256]{4,3,2,1,0:T(8,128)(2,1)} %v_hbm.1, f32[5,16,16,256]{3,2,1,0:T(8,128)} %base_hbm.1, s32[16,16,256]{2,1,0:T(8,128)} %cell_hbm.1, s32[16]{0:T(128)} %pick.1, f32[3,5,5]{2,1,0:T(8,128)} %copy.7.mix), custom_call_target="tpu_custom_call" | custom-call | tf_op jit(solution)/shard_map/pallas_call | solution.py:446
  94.8 2.5 %copy.9 = f32[5,16,16,256]{3,2,1,0:T(8,128)} copy(f32[5,16,16,256]{3,2,1,0:T(8,128)} %shard_map.64) | data formatting | bytes 2621440

commit v2 on v1

--- a/solution.py
+++ b/solution.py
@@ -46,9 +46,9 @@
     u_hbm, v_hbm, base_hbm, cell_hbm, pick, mix,
     out_hbm,
     u, v, base, cell, uface, vface, uhalo, wface, mats, mat2, mat0, select, circ,
-    w_scr, du_scr, acc, grad, sx, sface, shalo, ysend, yhalo, field, wall, base_dz, bface, bhalo,
+    w_scr, du_scr, acc, grad, sx, sx_all, sface, shalo, ysend, yhalo, field, wall, base_dz, bface, bhalo,
     fterm, energy, round_one, round_two, round_three, amp, weight, result,
-    load_sem, usend_sem, urecv_sem, xs_sem, xr_sem, ys_sem, yr_sem, es_sem, er_sem, out_sem,
+    load_sem, xs_sem, xr_sem, ys_sem, yr_sem, es_sem, er_sem, out_sem,
 ):
     nc, nn, modes, nv, nx, ny, nz = sizes
     kv = nv * ny
@@ -97,7 +97,7 @@
     def _():
         u[:, :, nx + 1] = jnp.zeros((modes, nv, ny, nz), BF16)
         base[:, nx + 1] = jnp.zeros((nv, ny, nz), F32)
-        sx[:, nx + 1] = jnp.zeros((nv, ny, nz), F32)
+        sx[:, 3] = jnp.zeros((nv, ny, nz), F32)
         field[0, :, nx + 1] = jnp.zeros((nv, ny, nz), F32)
         field[1, :, nx + 1] = jnp.zeros((nv, ny, nz), F32)
 
@@ -117,28 +117,25 @@
             src_ref=src, dst_ref=dst, send_sem=xs_sem.at[kind, way], recv_sem=xr_sem.at[kind, 1 - way],
             device_id=(lax.rem(c + step[way] + nc, nc), n), device_id_type=MESH)
 
-    def y_copy(send_sems, recv_sems, kind, way, src, dst):
+    def y_copy(kind, way, src, dst):
         return pltpu.make_async_remote_copy(
-            src_ref=src, dst_ref=dst, send_sem=send_sems.at[kind, way], recv_sem=recv_sems.at[kind, 1 - way],
+            src_ref=src, dst_ref=dst, send_sem=ys_sem.at[kind, way], recv_sem=yr_sem.at[kind, 1 - way],
             device_id=(c, lax.rem(n + step[way] + nn, nn)), device_id_type=MESH)
 
     x_links = [
         lambda w: x_copy(0, w, u_hbm.at[:, :, (nx - 1) * w], u.at[:, :, (nx + 1) * (1 - w)]),
         lambda w: x_copy(1, w, base_hbm.at[:, (nx - 1) * w], base.at[:, (nx + 1) * (1 - w)]),
-        lambda w: x_copy(2, w, sx.at[:, 1 + (nx - 1) * w], sx.at[:, (nx + 1) * (1 - w)]),
+        lambda w: x_copy(2, w, sx.at[:, 1 + w], sx.at[:, 3 * (1 - w)]),
         lambda w: x_copy(3, w, field.at[0, :, 1 + (nx - 1) * w], field.at[0, :, (nx + 1) * (1 - w)]),
         lambda w: x_copy(4, w, field.at[1, :, 1 + (nx - 1) * w], field.at[1, :, (nx + 1) * (1 - w)]),
     ]
     y_links = [
-        lambda w: y_copy(ys_sem, yr_sem, 0, w, bface.at[w], bhalo.at[1 - w]),
-        lambda w: y_copy(ys_sem, yr_sem, 1, w, sface.at[w], shalo.at[1 - w]),
-        lambda w: y_copy(ys_sem, yr_sem, 2, w, ysend.at[0, w], yhalo.at[0, 1 - w]),
-        lambda w: y_copy(ys_sem, yr_sem, 3, w, ysend.at[1, w], yhalo.at[1, 1 - w]),
+        lambda w: y_copy(0, w, bface.at[w], bhalo.at[1 - w]),
+        lambda w: y_copy(1, w, sface.at[w], shalo.at[1 - w]),
+        lambda w: y_copy(2, w, ysend.at[0, w], yhalo.at[0, 1 - w]),
+        lambda w: y_copy(3, w, ysend.at[1, w], yhalo.at[1, 1 - w]),
+        lambda w: y_copy(4, w, uface.at[w], uhalo.at[1 - w]),
     ]
-
-    def u_link(g):
-        s = pl.ds(g * GROUP, GROUP)
-        return lambda w: y_copy(usend_sem, urecv_sem, g, w, uface.at[w, s], uhalo.at[1 - w, s])
 
     def send(link, has):
         for w in (0, 1):
@@ -157,9 +154,6 @@
             @pl.when(has[w])
             def _():
                 link(w).wait_send()
-
-    send(x_links[0], has_x)
-    send(x_links[1], has_x)
 
     pick_row = iota((2 * nx, nx * ny), 0)
     from_row = iota((2 * nx, nx * ny), 1)
@@ -191,7 +185,6 @@
             return carry
 
         lax.fori_loop(g * GROUP, (g + 1) * GROUP, u_mode, 0)
-        send(u_link(g), has_y)
 
     def e_copy(index, peer, dst):
         return pltpu.make_async_remote_copy(
@@ -257,7 +250,6 @@
     for side in (0, 1):
         for x in range(nx):
             bface[side, :, pl.ds(x, 1), :] = base[:, 1 + x, pl.ds((ny - 1) * side, 1), :]
-    send(y_links[0], has_y)
 
     def base_plane(x, carry):
         for j in range(nv):
@@ -269,6 +261,10 @@
 
     cells_all = nc * nn * nv * nx * ny * nz
     total = jnp.sum(finish(threes, round_three, 2), axis=1, keepdims=True)
+    send(x_links[0], has_x)
+    send(y_links[4], has_y)
+    send(x_links[1], has_x)
+    send(y_links[0], has_y)
     amp[...] = jnp.broadcast_to(lax.rsqrt(total / cells_all + 1e-06) / modes, amp.shape)
 
     def mode_matrix(m, carry):
@@ -281,70 +277,86 @@
 
     sface[...] = jnp.zeros(sface.shape, F32)
     sx[:, 1] = jnp.zeros((nv, ny, nz), F32)
-    sx[:, nx] = jnp.zeros((nv, ny, nz), F32)
-
-    def face_mode(m, carry):
-        p = pick[m]
+    sx[:, 2] = jnp.zeros((nv, ny, nz), F32)
+
+    def face_group(g, carry):
+        m0 = g * GROUP
         for s in (0, 1):
-            rows = vface[s, p].reshape(kv, nz)
-            w = dot(mats[m, pl.ds(4 * kv, kv), :], jnp.concatenate([rows, rows], axis=0))
-            wface[s, m] = w
-            sface[s] += w.reshape(nv, nx, nz) * uface[s, m].astype(F32)
-            rows = v[p, :, (nx - 1) * s].reshape(kv, nz)
-            w = dot(mats[m, pl.ds(0, kv), :], jnp.concatenate([rows, rows], axis=0))
             x = 1 + (nx - 1) * s
-            sx[:, x] += w.reshape(nv, ny, nz) * u[m, :, x].astype(F32)
+            for k in range(GROUP):
+                rows = vface[s, pick[m0 + k]].reshape(kv, nz)
+                wface[s, m0 + k] = dot(mats[m0 + k, pl.ds(4 * kv, kv), :], jnp.concatenate([rows, rows], axis=0))
+                rows = v[pick[m0 + k], :, x - 1].reshape(kv, nz)
+                w_scr[s, k, pl.ds(0, kv), :] = dot(mats[m0 + k, pl.ds(0, kv), :], jnp.concatenate([rows, rows], axis=0))
+        for s in (0, 1):
+            x = 1 + (nx - 1) * s
+            for j in range(nv):
+                r = pl.ds(j * ny, ny)
+                at_face, at_end = sface[s, j], sx[j, 1 + s]
+                for k in range(GROUP):
+                    at_face = at_face + wface[s, m0 + k, pl.ds(j * nx, nx), :] * uface[s, m0 + k, j].astype(F32)
+                    at_end = at_end + w_scr[s, k, r, :] * u[m0 + k, j, x].astype(F32)
+                sface[s, j] = at_face
+                sx[j, 1 + s] = at_end
         return carry
 
-    lax.fori_loop(0, modes, face_mode, 0)
+    lax.fori_loop(0, groups, face_group, 0)
     send(x_links[2], has_x)
     send(y_links[1], has_y)
 
-    def plane(x):
-        def group(g, carry):
-            m0 = g * GROUP
-            du_scr[...] = dot(u[pl.ds(m0, GROUP), :, x].reshape(GROUP * kv, nz), circ[...])
-            for k in range(GROUP):
-                rows = v[pick[m0 + k], :, x - 1].reshape(kv, nz)
-                w_scr[k] = dot(mats[m0 + k, pl.ds(0, 4 * kv), :], jnp.concatenate([rows, rows], axis=0))
+    def mix_part(x, g, slot, k):
+        m0 = g * GROUP
+        if k == GROUP:
+            du_scr[slot] = dot(u[pl.ds(m0, GROUP), :, x].reshape(GROUP * kv, nz), circ[...])
+        elif k < GROUP:
+            rows = v[pick[m0 + k], :, x - 1].reshape(kv, nz)
+            w_scr[slot, k] = dot(mats[m0 + k, pl.ds(0, 4 * kv), :], jnp.concatenate([rows, rows], axis=0))
+
+    def mix_group(x, g, slot):
+        for k in range(GROUP + 1):
+            mix_part(x, g, slot, k)
+
+    def plane_of(t):
+        return lax.rem(t + 1, nx) + 1
+
+    def plane(t, carry):
+        x = plane_of(t)
+        for g in range(groups):
+            slot = g % 2
             for j in range(nv):
-                q, s_x, s_z, up, down = (acc[t, j] for t in range(5))
+                if g < groups - 1:
+                    mix_part(x, g + 1, 1 - slot, j)
+                else:
+                    mix_part(plane_of(t + 1), 0, 1 - slot, j)
+                if g == 0:
+                    q = s_x = s_z = up = down = jnp.zeros((ny, nz), F32)
+                else:
+                    q, s_x, s_z, up, down = (acc[i, j] for i in range(5))
                 for k in range(GROUP):
-                    here = u[m0 + k, j, x].astype(F32)
-                    dx = u[m0 + k, j, x + 1].astype(F32) - u[m0 + k, j, x - 1].astype(F32)
-                    dz = du_scr[pl.ds(k * kv + j * ny, ny), :]
-                    wx, wp, wm, wz = (w_scr[k, pl.ds(t * kv + j * ny, ny), :] for t in range(4))
+                    m = g * GROUP + k
+                    here = u[m, j, x].astype(F32)
+                    dx = u[m, j, x + 1].astype(F32) - u[m, j, x - 1].astype(F32)
+                    dz = du_scr[slot, pl.ds(k * kv + j * ny, ny), :]
+                    wx, wp, wm, wz = (w_scr[slot, k, pl.ds(i * kv + j * ny, ny), :] for i in range(4))
                     q = q + dx * wx + dz * wz
                     s_x = s_x + here * wx
                     s_z = s_z + here * wz
                     up = up + here * wm
                     down = down + here * wp
-                for t, value in enumerate((q, s_x, s_z, up, down)):
-                    acc[t, j] = value
-            return carry
-
-        acc[...] = jnp.zeros(acc.shape, F32)
-        lax.fori_loop(0, groups, group, 0)
-        for j in range(nv):
-            grad[j, x - 1] = acc[0, j] - diff_lanes(acc[2, j]) - rows_up(acc[3, j]) - rows_down(acc[4, j])
-
-    def inner_plane(x, carry):
-        plane(x)
-        for j in range(nv):
-            sx[j, x] = acc[1, j]
+                if g < groups - 1:
+                    for i, value in enumerate((q, s_x, s_z, up, down)):
+                        acc[i, j] = value
+                else:
+                    grad[j, x - 1] = q - diff_lanes(s_z) - rows_up(up) - rows_down(down)
+                    sx_all[j, x - 1] = s_x
         return carry
 
-    lax.fori_loop(2, nx, inner_plane, 0)
+    mix_group(plane_of(0), 0, 0)
+    lax.fori_loop(0, nx - 2, plane, 0)
     receive(x_links[0], has_x)
-
-    def end_plane(s, carry):
-        plane(1 + (nx - 1) * s)
-        return carry
-
-    lax.fori_loop(0, 2, end_plane, 0)
-
-    for g in range(groups):
-        receive(u_link(g), has_y)
+    lax.fori_loop(nx - 2, nx, plane, 0)
+
+    receive(y_links[4], has_y)
     fterm[...] = jnp.zeros(fterm.shape, F32)
 
     def cross_mode(m, carry):
@@ -366,10 +378,13 @@
 
     def grad_plane(x, carry):
         for j in range(nv):
-            grad[j, x] = grad[j, x] - (sx[j, x + 2] - sx[j, x])
+            grad[j, x] = grad[j, x] - (sx_all[j, x + 1] - sx_all[j, x - 1])
         return carry
 
-    lax.fori_loop(0, nx, grad_plane, 0)
+    for j in range(nv):
+        grad[j, 0] = grad[j, 0] - (sx_all[j, 1] - sx[j, 0])
+        grad[j, nx - 1] = grad[j, nx - 1] - (sx[j, 3] - sx_all[j, nx - 2])
+    lax.fori_loop(1, nx - 1, grad_plane, 0, unroll=2)
     add_rows(grad, 0)
 
     def apply(slot, source, target):
@@ -378,18 +393,19 @@
                 field[slot, j, x + 1] = weight[x] * source[j, x]
             return carry
 
-        lax.fori_loop(0, nx, weigh, 0)
+        lax.fori_loop(0, nx, weigh, 0, unroll=2)
         for side in (0, 1):
             for x in range(nx):
                 ysend[slot, side, :, pl.ds(x, 1), :] = field[slot, :, 1 + x, pl.ds((ny - 1) * side, 1), :]
         send(x_links[3 + slot], has_x)
         send(y_links[2 + slot], has_y)
 
+
         def mixed(x, carry):
             wall[x] = dot(mat2[pl.ds(0, 4 * kv), :], split3(field[slot, :, x].reshape(kv, nz)))
             return carry
 
-        lax.fori_loop(1, nx + 1, mixed, 0)
+        lax.fori_loop(1, nx + 1, mixed, 0, unroll=4)
         own = [dot(mat2[pl.ds(4 * kv, kv), :], split3(ysend[slot, s].reshape(kv, nz))) for s in (0, 1)]
         for s in (0, 1):
             wface[s, 0] = own[s]
@@ -405,7 +421,7 @@
                 target[j, x - 1] = value - rows_up(here * wm) - rows_down(here * wp)
             return carry
 
-        lax.fori_loop(2, nx, result_plane, 0)
+        lax.fori_loop(2, nx, result_plane, 0, unroll=2)
         if slot == 0:
             receive(x_links[1], has_x)
             receive(y_links[0], has_y)
@@ -413,7 +429,7 @@
         receive(y_links[2 + slot], has_y)
         for x in (0, nx + 1):
             wall[x, pl.ds(0, kv), :] = dot(mat2[pl.ds(0, kv), :], split3(field[slot, :, x].reshape(kv, nz)))
-        lax.fori_loop(0, 2, lambda s, carry: result_plane(1 + (nx - 1) * s, carry), 0)
+        lax.fori_loop(0, 2, lambda s, carry: result_plane(1 + (nx - 1) * s, carry), 0, unroll=2)
         for s in (0, 1):
             far = dot(mat2[pl.ds(4 * kv, kv), :], split3(yhalo[slot, s].reshape(kv, nz)))
             change = (far - wface[s, 0]).reshape(nv, nx, nz) * bhalo[s]
@@ -424,8 +440,6 @@
     apply(1, result, grad)
     store = pltpu.make_async_copy(grad, out_hbm, out_sem)
     store.start()
-    for g in range(groups):
-        drain(u_link(g), has_y)
     for link in x_links:
         drain(link, has_x)
     for link in y_links:
@@ -462,11 +476,12 @@
             vm((5 * kv, 3 * kv), F32),
             vm((2 * nx, nx * ny), BF16),
             vm((nz, nz), BF16),
-            vm((GROUP, 4 * kv, nz), F32),
-            vm((GROUP * kv, nz), F32),
+            vm((2, GROUP, 4 * kv, nz), F32),
+            vm((2, GROUP * kv, nz), F32),
             vm((5, nv, ny, nz), F32),
             vm((nv, nx, ny, nz), F32),
-            vm((nv, nx + 2, ny, nz), F32),
+            vm((nv, 4, ny, nz), F32),
+            vm((nv, nx, ny, nz), F32),
             vm((2, nv, nx, nz), F32),
             vm((2, nv, nx, nz), F32),
             vm((2, 2, nv, nx, nz), F32),
@@ -485,12 +500,10 @@
             vm((nx, ny, nz), F32),
             vm((nv, nx, ny, nz), F32),
             pltpu.SemaphoreType.DMA((2 * groups + 2,)),
-            pltpu.SemaphoreType.DMA((groups, 2)),
-            pltpu.SemaphoreType.DMA((groups, 2)),
             pltpu.SemaphoreType.DMA((5, 2)),
             pltpu.SemaphoreType.DMA((5, 2)),
-            pltpu.SemaphoreType.DMA((4, 2)),
-            pltpu.SemaphoreType.DMA((4, 2)),
+            pltpu.SemaphoreType.DMA((5, 2)),
+            pltpu.SemaphoreType.DMA((5, 2)),
             pltpu.SemaphoreType.DMA((nc + nn // 4 + 1,)),
             pltpu.SemaphoreType.DMA((nc + nn // 4 + 1,)),
             pltpu.SemaphoreType.DMA,

time: 97.6 us -> 73.8 us (0.76)
  Pallas kernels: 93.5 us -> 69.7 us
    pallas_call x1, Pallas kernels: 93.5 us -> 69.7 us  [per_device(): pl.pallas_call(functools.partial(kernel, (nc, nn, modes, nv, nx, ny, nz))...]
where the time goes in v2:
time: 73.8 us; the launch traced here: 73.6 us
  Pallas kernels  69.7 us (94%)
  local copies, waits for them, and re-layouts  3.82 us (5%)
    pallas_call x1, Pallas kernels, per_device(): pl.pallas_call(functools.partial(kernel, (nc, nn, modes, nv, nx, ny, nz))...  69.7 us
    unnamed x2, local copies, waits for them, and re-layouts  3.82 us

profile of v2, /device:TPU:6, one launch (start us, length us, event | category | flops | bytes accessed | tf_op | source)
XLA Modules:
  0.0 73.6 jit_solution(10423851411690572163)
XLA Ops:
  0.0 1.3 %copy.7.mix = f32[3,5,5]{2,1,0:T(8,128)} copy(f32[3,5,5]{2,0,1:T(4,128)} %param.11) | data formatting | bytes 600 | tf_op args[5]
  1.3 69.7 %shard_map.64 = f32[5,16,16,256]{3,2,1,0:T(8,128)} custom-call(bf16[16,5,16,16,256]{4,3,2,1,0:T(8,128)(2,1)} %u_hbm.1, bf16[16,5,16,16,256]{4,3,2,1,0:T(8,128)(2,1)} %v_hbm.1, f32[5,16,16,256]{3,2,1,0:T(8,128)} %base_hbm.1, s32[16,16,256]{2,1,0:T(8,128)} %cell_hbm.1, s32[16]{0:T(128)} %pick.1, f32[3,5,5]{2,1,0:T(8,128)} %copy.7.mix), custom_call_target="tpu_custom_call" | custom-call | tf_op jit(solution)/shard_map/pallas_call | solution.py:460
  71.0 2.5 %copy.9 = f32[5,16,16,256]{3,2,1,0:T(8,128)} copy(f32[5,16,16,256]{3,2,1,0:T(8,128)} %shard_map.64) | data formatting | bytes 2621440

commit v3 on v2

--- a/solution.py
+++ b/solution.py
@@ -11,6 +11,7 @@
 F32 = jnp.float32
 BF16 = jnp.bfloat16
 GROUP = 4
+MG = 2
 
 
 def iota(shape, dim):
@@ -43,9 +44,9 @@
 
 def kernel(
     sizes,
-    u_hbm, v_hbm, base_hbm, cell_hbm, pick, mix,
+    u_hbm, v_hbm, base_hbm, cell_hbm, mix_hbm, pick,
     out_hbm,
-    u, v, base, cell, uface, vface, uhalo, wface, mats, mat2, mat0, select, circ,
+    u, v, base, cell, mix, uface, vface, uhalo, wface, mats, mat2, mat0, select, circ,
     w_scr, du_scr, acc, grad, sx, sx_all, sface, shalo, ysend, yhalo, field, wall, base_dz, bface, bhalo,
     fterm, energy, round_one, round_two, round_three, amp, weight, result,
     load_sem, xs_sem, xr_sem, ys_sem, yr_sem, es_sem, er_sem, out_sem,
@@ -55,6 +56,9 @@
     c, n = lax.axis_index("chord"), lax.axis_index("normal")
     has_x = (c > 0, c < nc - 1)
     has_y = (n > 0, n < nn - 1)
+    half = nn // 2
+    far_y = (n == half, n == half - 1)
+    near_y = tuple(jnp.logical_and(a, jnp.logical_not(b)) for a, b in zip(has_y, far_y))
     step = (-1, 1)
     zs, rest = 4, nn // 4
     groups = modes // GROUP
@@ -69,6 +73,8 @@
 
     base_load = pltpu.make_async_copy(base_hbm, base.at[:, pl.ds(1, nx)], load_sem.at[2 * groups])
     cell_load = pltpu.make_async_copy(cell_hbm, cell, load_sem.at[2 * groups + 1])
+    mix_load = pltpu.make_async_copy(mix_hbm, mix, load_sem.at[2 * groups + 2])
+    mix_load.start()
     for g in range(groups):
         u_load(g).start()
     base_load.start()
@@ -134,7 +140,8 @@
         lambda w: y_copy(1, w, sface.at[w], shalo.at[1 - w]),
         lambda w: y_copy(2, w, ysend.at[0, w], yhalo.at[0, 1 - w]),
         lambda w: y_copy(3, w, ysend.at[1, w], yhalo.at[1, 1 - w]),
-        lambda w: y_copy(4, w, uface.at[w], uhalo.at[1 - w]),
+        lambda w: y_copy(4, w, uface.at[w, pl.ds(0, GROUP)], uhalo.at[1 - w, pl.ds(0, GROUP)]),
+        lambda w: y_copy(5, w, uface.at[w, pl.ds(GROUP, modes - GROUP)], uhalo.at[1 - w, pl.ds(GROUP, modes - GROUP)]),
     ]
 
     def send(link, has):
@@ -185,6 +192,8 @@
             return carry
 
         lax.fori_loop(g * GROUP, (g + 1) * GROUP, u_mode, 0)
+        if g == 0:
+            send(y_links[4], far_y)
 
     def e_copy(index, peer, dst):
         return pltpu.make_async_remote_copy(
@@ -202,7 +211,7 @@
             faces_of(lambda m, i: v[m, i], vface, m)
             return carry
 
-        lax.fori_loop(g * GROUP, (g + 1) * GROUP, v_mode, 0)
+        lax.fori_loop(g * GROUP, (g + 1) * GROUP, v_mode, 0, unroll=2)
 
     def finish(copies, slots, src):
         total = energy[pl.ds(modes * src, modes), :]
@@ -218,6 +227,7 @@
     for copy in twos:
         copy.start()
 
+    mix_load.wait()
     width = 3 * kv
     lane = iota((ny, width), 1)
     row = iota((ny, width), 0)
@@ -227,11 +237,12 @@
     nxt = jnp.where(lane_row == row + 1, 1.0, 0.0)
     prv = jnp.where(lane_row == row - 1, 1.0, 0.0)
     kinds = ((0, same), (1, nxt - same), (1, same - prv), (2, same), (1, same))
+    table = [mix[i] for i in range(nv)]
     for k, (d, stencil) in enumerate(kinds):
         for j in range(nv):
             coefs = jnp.zeros((ny, width), F32)
             for i in range(nv):
-                coefs = jnp.where(lane_var == i, mix[d, i, j], coefs)
+                coefs = jnp.where(lane_var == i, table[i][d : d + 1, j : j + 1], coefs)
             mat0[pl.ds((k * nv + j) * ny, ny), :] = coefs * stencil
     high = mat0[...].astype(BF16)
     low = (mat0[...] - high.astype(F32)).astype(BF16)
@@ -261,8 +272,10 @@
 
     cells_all = nc * nn * nv * nx * ny * nz
     total = jnp.sum(finish(threes, round_three, 2), axis=1, keepdims=True)
+    send(y_links[5], far_y)
     send(x_links[0], has_x)
-    send(y_links[4], has_y)
+    send(y_links[4], near_y)
+    send(y_links[5], near_y)
     send(x_links[1], has_x)
     send(y_links[0], has_y)
     amp[...] = jnp.broadcast_to(lax.rsqrt(total / cells_all + 1e-06) / modes, amp.shape)
@@ -305,15 +318,15 @@
     send(y_links[1], has_y)
 
     def mix_part(x, g, slot, k):
-        m0 = g * GROUP
-        if k == GROUP:
-            du_scr[slot] = dot(u[pl.ds(m0, GROUP), :, x].reshape(GROUP * kv, nz), circ[...])
-        elif k < GROUP:
+        m0 = g * MG
+        if k == MG:
+            du_scr[slot] = dot(u[pl.ds(m0, MG), :, x].reshape(MG * kv, nz), circ[...])
+        elif k < MG:
             rows = v[pick[m0 + k], :, x - 1].reshape(kv, nz)
             w_scr[slot, k] = dot(mats[m0 + k, pl.ds(0, 4 * kv), :], jnp.concatenate([rows, rows], axis=0))
 
     def mix_group(x, g, slot):
-        for k in range(GROUP + 1):
+        for k in range(MG + 1):
             mix_part(x, g, slot, k)
 
     def plane_of(t):
@@ -321,34 +334,36 @@
 
     def plane(t, carry):
         x = plane_of(t)
-        for g in range(groups):
+        for g in range((modes // MG)):
             slot = g % 2
             for j in range(nv):
-                if g < groups - 1:
-                    mix_part(x, g + 1, 1 - slot, j)
-                else:
-                    mix_part(plane_of(t + 1), 0, 1 - slot, j)
-                if g == 0:
-                    q = s_x = s_z = up = down = jnp.zeros((ny, nz), F32)
-                else:
-                    q, s_x, s_z, up, down = (acc[i, j] for i in range(5))
-                for k in range(GROUP):
-                    m = g * GROUP + k
-                    here = u[m, j, x].astype(F32)
-                    dx = u[m, j, x + 1].astype(F32) - u[m, j, x - 1].astype(F32)
-                    dz = du_scr[slot, pl.ds(k * kv + j * ny, ny), :]
-                    wx, wp, wm, wz = (w_scr[slot, k, pl.ds(i * kv + j * ny, ny), :] for i in range(4))
-                    q = q + dx * wx + dz * wz
-                    s_x = s_x + here * wx
-                    s_z = s_z + here * wz
-                    up = up + here * wm
-                    down = down + here * wp
-                if g < groups - 1:
+                for part in range(j, MG + 1, nv):
+                    if g < (modes // MG) - 1:
+                        mix_part(x, g + 1, 1 - slot, part)
+                    else:
+                        mix_part(plane_of(t + 1), 0, 1 - slot, part)
+                for h in (0, 1):
+                    z = pl.ds(128 * h, 128)
+                    if g == 0:
+                        q = s_x = s_z = up = down = jnp.zeros((ny, 128), F32)
+                    else:
+                        q, s_x, s_z, up, down = (acc[i, j, :, z] for i in range(5))
+                    for k in range(MG):
+                        m = g * MG + k
+                        here = u[m, j, x, :, z].astype(F32)
+                        dx = u[m, j, x + 1, :, z].astype(F32) - u[m, j, x - 1, :, z].astype(F32)
+                        dz = du_scr[slot, pl.ds(k * kv + j * ny, ny), z]
+                        wx, wp, wm, wz = (w_scr[slot, k, pl.ds(i * kv + j * ny, ny), z] for i in range(4))
+                        q = q + dx * wx + dz * wz
+                        s_x = s_x + here * wx
+                        s_z = s_z + here * wz
+                        up = up + here * wm
+                        down = down + here * wp
                     for i, value in enumerate((q, s_x, s_z, up, down)):
-                        acc[i, j] = value
-                else:
-                    grad[j, x - 1] = q - diff_lanes(s_z) - rows_up(up) - rows_down(down)
-                    sx_all[j, x - 1] = s_x
+                        acc[i, j, :, z] = value
+                if g == (modes // MG) - 1:
+                    grad[j, x - 1] = acc[0, j] - diff_lanes(acc[2, j]) - rows_up(acc[3, j]) - rows_down(acc[4, j])
+                    sx_all[j, x - 1] = acc[1, j]
         return carry
 
     mix_group(plane_of(0), 0, 0)
@@ -357,6 +372,7 @@
     lax.fori_loop(nx - 2, nx, plane, 0)
 
     receive(y_links[4], has_y)
+    receive(y_links[5], has_y)
     fterm[...] = jnp.zeros(fterm.shape, F32)
 
     def cross_mode(m, carry):
@@ -460,13 +476,14 @@
     return pl.pallas_call(
         functools.partial(kernel, (nc, nn, modes, nv, nx, ny, nz)),
         out_shape=jax.ShapeDtypeStruct(base.shape, F32),
-        in_specs=[any_space] * 4 + [smem] * 2,
+        in_specs=[any_space] * 5 + [smem],
         out_specs=any_space,
         scratch_shapes=[
             vm((modes, nv, nx + 2, ny, nz), BF16),
             vm((modes, nv, nx, ny, nz), BF16),
             vm((nv, nx + 2, ny, nz), F32),
             vm((nx, ny, nz), jnp.int32),
+            vm((nv, 3, nv), F32),
             vm((2, modes, nv, nx, nz), BF16),
             vm((2, modes, nv, nx, nz), BF16),
             vm((2, modes, nv, nx, nz), BF16),
@@ -476,8 +493,8 @@
             vm((5 * kv, 3 * kv), F32),
             vm((2 * nx, nx * ny), BF16),
             vm((nz, nz), BF16),
-            vm((2, GROUP, 4 * kv, nz), F32),
-            vm((2, GROUP * kv, nz), F32),
+            vm((2, max(GROUP, MG), 4 * kv, nz), F32),
+            vm((2, MG * kv, nz), F32),
             vm((5, nv, ny, nz), F32),
             vm((nv, nx, ny, nz), F32),
             vm((nv, 4, ny, nz), F32),
@@ -499,18 +516,18 @@
             vm((modes, 256), F32),
             vm((nx, ny, nz), F32),
             vm((nv, nx, ny, nz), F32),
-            pltpu.SemaphoreType.DMA((2 * groups + 2,)),
+            pltpu.SemaphoreType.DMA((2 * groups + 3,)),
             pltpu.SemaphoreType.DMA((5, 2)),
             pltpu.SemaphoreType.DMA((5, 2)),
-            pltpu.SemaphoreType.DMA((5, 2)),
-            pltpu.SemaphoreType.DMA((5, 2)),
+            pltpu.SemaphoreType.DMA((6, 2)),
+            pltpu.SemaphoreType.DMA((6, 2)),
             pltpu.SemaphoreType.DMA((nc + nn // 4 + 1,)),
             pltpu.SemaphoreType.DMA((nc + nn // 4 + 1,)),
             pltpu.SemaphoreType.DMA,
         ],
         compiler_params=pltpu.CompilerParams(
             collective_id=0, has_side_effects=True, vmem_limit_bytes=60 * 2**20),
-    )(u, v, base, cell, pick, mix)
+    )(u, v, base, cell, mix.transpose(1, 0, 2), pick)
 
 
 def solution(mesh):

time: 73.8 us -> 68.5 us (0.928)
  Pallas kernels: 69.7 us -> 65.8 us
  local copies, waits for them, and re-layouts: 3.82 us -> 2.52 us
    pallas_call x1, Pallas kernels: 69.7 us -> 65.8 us  [per_device(): pl.pallas_call(functools.partial(kernel, (nc, nn, modes, nv, nx, ny, nz))...]
    unnamed x2 -> x1, local copies, waits for them, and re-layouts: 3.82 us -> 2.52 us
where the time goes in v3:
time: 68.5 us; the launch traced here: 68.4 us
  Pallas kernels  65.8 us (96%)
  local copies, waits for them, and re-layouts  2.52 us (4%)
    pallas_call x1, Pallas kernels, per_device(): pl.pallas_call(functools.partial(kernel, (nc, nn, modes, nv, nx, ny, nz))...  65.8 us
    unnamed x1, local copies, waits for them, and re-layouts  2.52 us

profile of v3, /device:TPU:6, one launch (start us, length us, event | category | flops | bytes accessed | tf_op | source)
XLA Modules:
  0.0 68.4 jit_solution(9946915515066973167)
XLA Ops:
  0.0 65.8 %shard_map.64 = f32[5,16,16,256]{3,2,1,0:T(8,128)} custom-call(bf16[16,5,16,16,256]{4,3,2,1,0:T(8,128)(2,1)} %u_hbm.1, bf16[16,5,16,16,256]{4,3,2,1,0:T(8,128)(2,1)} %v_hbm.1, f32[5,16,16,256]{3,2,1,0:T(8,128)} %base_hbm.1, s32[16,16,256]{2,1,0:T(8,128)} %cell_hbm.1, f32[5,3,5]{2,1,0:T(4,128)} %bitcast.1, s32[16]{0:T(128)} %pick.1), custom_call_target="tpu_custom_call" | custom-call | tf_op jit(solution)/shard_map/pallas_call | solution.py:476
  65.8 2.5 %copy.8 = f32[5,16,16,256]{3,2,1,0:T(8,128)} copy(f32[5,16,16,256]{3,2,1,0:T(8,128)} %shard_map.64) | data formatting | bytes 2621440

commit v4 on v3

--- a/solution.py
+++ b/solution.py
@@ -48,8 +48,8 @@
     out_hbm,
     u, v, base, cell, mix, uface, vface, uhalo, wface, mats, mat2, mat0, select, circ,
     w_scr, du_scr, acc, grad, sx, sx_all, sface, shalo, ysend, yhalo, field, wall, base_dz, bface, bhalo,
-    fterm, energy, round_one, round_two, round_three, amp, weight, result,
-    load_sem, xs_sem, xr_sem, ys_sem, yr_sem, es_sem, er_sem, out_sem,
+    fterm, relay, energy, round_one, round_two, round_three, amp, weight, result,
+    load_sem, xs_sem, xr_sem, ys_sem, yr_sem, relay_send, relay_recv, es_sem, er_sem, out_sem,
 ):
     nc, nn, modes, nv, nx, ny, nz = sizes
     kv = nv * ny
@@ -85,7 +85,7 @@
     first = [(lax.rem(c + k, nc), n) for k in range(1, nc)]
     second = [(c, n // zs * zs + lax.rem(lax.rem(n, zs) + k, zs)) for k in range(1, zs)]
     third = [(c, lax.rem(n // zs + k, rest) * zs + lax.rem(n, zs)) for k in range(1, rest)]
-    around = [(c, lax.rem(n + 1, nn)), (c, lax.rem(n + nn - 1, nn))]
+    around = [(k, lax.rem(n + nn + d, nn)) for k in (c, lax.rem(c + nc // 2, nc)) for d in (1, -1)]
     barrier = pltpu.get_barrier_semaphore()
     peers = first + second + third + around
     for peer in peers:
@@ -127,6 +127,8 @@
         return pltpu.make_async_remote_copy(
             src_ref=src, dst_ref=dst, send_sem=ys_sem.at[kind, way], recv_sem=yr_sem.at[kind, 1 - way],
             device_id=(c, lax.rem(n + step[way] + nn, nn)), device_id_type=MESH)
+
+    late = pl.ds(2 * GROUP, modes - 2 * GROUP)
 
     x_links = [
         lambda w: x_copy(0, w, u_hbm.at[:, :, (nx - 1) * w], u.at[:, :, (nx + 1) * (1 - w)]),
@@ -141,8 +143,28 @@
         lambda w: y_copy(2, w, ysend.at[0, w], yhalo.at[0, 1 - w]),
         lambda w: y_copy(3, w, ysend.at[1, w], yhalo.at[1, 1 - w]),
         lambda w: y_copy(4, w, uface.at[w, pl.ds(0, GROUP)], uhalo.at[1 - w, pl.ds(0, GROUP)]),
-        lambda w: y_copy(5, w, uface.at[w, pl.ds(GROUP, modes - GROUP)], uhalo.at[1 - w, pl.ds(GROUP, modes - GROUP)]),
+        lambda w: y_copy(5, w, uface.at[w, pl.ds(GROUP, GROUP)], uhalo.at[1 - w, pl.ds(GROUP, GROUP)]),
+        lambda w: y_copy(6, w, uface.at[w, late], uhalo.at[1 - w, late]),
     ]
+
+    upper = c // (nc // 2)
+    other = lax.rem(c + nc // 2, nc)
+
+    def relay_copy(hop, w):
+        across = lax.rem(n + step[w] * (1 - upper) + nn, nn)
+        if hop == 0:
+            src, dst = uface.at[w, late], relay
+        else:
+            src, dst = relay, uhalo.at[upper * w + (1 - upper) * (1 - w), late]
+        return pltpu.make_async_remote_copy(
+            src_ref=src, dst_ref=dst, send_sem=relay_send.at[hop], recv_sem=relay_recv.at[hop],
+            device_id=(other, across), device_id_type=MESH)
+
+    def relay_receive(hop, w):
+        dst = relay if hop == 0 else uhalo.at[w, late]
+        pltpu.make_async_remote_copy(
+            src_ref=relay, dst_ref=dst, send_sem=relay_send.at[hop], recv_sem=relay_recv.at[hop],
+            device_id=(other, n), device_id_type=MESH).wait_recv()
 
     def send(link, has):
         for w in (0, 1):
@@ -272,10 +294,16 @@
 
     cells_all = nc * nn * nv * nx * ny * nz
     total = jnp.sum(finish(threes, round_three, 2), axis=1, keepdims=True)
+    for w in (0, 1):
+        @pl.when(far_y[w])
+        def _():
+            relay_copy(0, w).start()
+
     send(y_links[5], far_y)
     send(x_links[0], has_x)
     send(y_links[4], near_y)
     send(y_links[5], near_y)
+    send(y_links[6], near_y)
     send(x_links[1], has_x)
     send(y_links[0], has_y)
     amp[...] = jnp.broadcast_to(lax.rsqrt(total / cells_all + 1e-06) / modes, amp.shape)
@@ -367,12 +395,25 @@
         return carry
 
     mix_group(plane_of(0), 0, 0)
-    lax.fori_loop(0, nx - 2, plane, 0)
+    lax.fori_loop(0, nx // 2, plane, 0)
+    for w in (0, 1):
+        @pl.when(far_y[w])
+        def _():
+            relay_receive(0, w)
+            relay_copy(1, w).start()
+
+    lax.fori_loop(nx // 2, nx - 2, plane, 0)
     receive(x_links[0], has_x)
     lax.fori_loop(nx - 2, nx, plane, 0)
 
     receive(y_links[4], has_y)
     receive(y_links[5], has_y)
+    receive(y_links[6], near_y)
+    for w in (0, 1):
+        @pl.when(far_y[w])
+        def _():
+            relay_receive(1, w)
+
     fterm[...] = jnp.zeros(fterm.shape, F32)
 
     def cross_mode(m, carry):
@@ -458,8 +499,15 @@
     store.start()
     for link in x_links:
         drain(link, has_x)
-    for link in y_links:
+    for link in y_links[:6]:
         drain(link, has_y)
+    drain(y_links[6], near_y)
+    for w in (0, 1):
+        @pl.when(far_y[w])
+        def _():
+            relay_copy(0, w).wait_send()
+            relay_copy(1, w).wait_send()
+
     for copy in ones + twos + threes:
         copy.wait_send()
     store.wait()
@@ -509,6 +557,7 @@
             vm((2, nv, nx, nz), F32),
             vm((2, nv, nx, nz), F32),
             vm((2, nv, nx, nz), F32),
+            vm((modes - 2 * GROUP, nv, nx, nz), BF16),
             vm((3 * modes, 128), F32),
             vm((nc - 1, modes, 128), F32),
             vm((3, modes, 128), F32),
@@ -519,8 +568,10 @@
             pltpu.SemaphoreType.DMA((2 * groups + 3,)),
             pltpu.SemaphoreType.DMA((5, 2)),
             pltpu.SemaphoreType.DMA((5, 2)),
-            pltpu.SemaphoreType.DMA((6, 2)),
-            pltpu.SemaphoreType.DMA((6, 2)),
+            pltpu.SemaphoreType.DMA((7, 2)),
+            pltpu.SemaphoreType.DMA((7, 2)),
+            pltpu.SemaphoreType.DMA((2,)),
+            pltpu.SemaphoreType.DMA((2,)),
             pltpu.SemaphoreType.DMA((nc + nn // 4 + 1,)),
             pltpu.SemaphoreType.DMA((nc + nn // 4 + 1,)),
             pltpu.SemaphoreType.DMA,

time: 68.5 us -> 72.9 us (1.064)
  Pallas kernels: 65.8 us -> 70.2 us
    pallas_call x1, Pallas kernels: 65.8 us -> 70.2 us  [per_device(): pl.pallas_call(functools.partial(kernel, (nc, nn, modes, nv, nx, ny, nz))...]
where the time goes in v4:
time: 72.9 us; the launch traced here: 72.8 us
  Pallas kernels  70.2 us (96%)
  local copies, waits for them, and re-layouts  2.52 us (3%)
    pallas_call x1, Pallas kernels, per_device(): pl.pallas_call(functools.partial(kernel, (nc, nn, modes, nv, nx, ny, nz))...  70.2 us
    unnamed x1, local copies, waits for them, and re-layouts  2.52 us

profile of v4, /device:TPU:6, one launch (start us, length us, event | category | flops | bytes accessed | tf_op | source)
XLA Modules:
  0.0 72.8 jit_solution(5723797083720418031)
XLA Ops:
  0.0 70.2 %shard_map.64 = f32[5,16,16,256]{3,2,1,0:T(8,128)} custom-call(bf16[16,5,16,16,256]{4,3,2,1,0:T(8,128)(2,1)} %u_hbm.1, bf16[16,5,16,16,256]{4,3,2,1,0:T(8,128)(2,1)} %v_hbm.1, f32[5,16,16,256]{3,2,1,0:T(8,128)} %base_hbm.1, s32[16,16,256]{2,1,0:T(8,128)} %cell_hbm.1, f32[5,3,5]{2,1,0:T(4,128)} %bitcast.1, s32[16]{0:T(128)} %pick.1), custom_call_target="tpu_custom_call" | custom-call | tf_op jit(solution)/shard_map/pallas_call | solution.py:524
  70.2 2.5 %copy.8 = f32[5,16,16,256]{3,2,1,0:T(8,128)} copy(f32[5,16,16,256]{3,2,1,0:T(8,128)} %shard_map.64) | data formatting | bytes 2621440

commit v5 on v3

--- a/solution.py
+++ b/solution.py
@@ -48,7 +48,7 @@
     out_hbm,
     u, v, base, cell, mix, uface, vface, uhalo, wface, mats, mat2, mat0, select, circ,
     w_scr, du_scr, acc, grad, sx, sx_all, sface, shalo, ysend, yhalo, field, wall, base_dz, bface, bhalo,
-    fterm, energy, round_one, round_two, round_three, amp, weight, result,
+    fterm, energy, round_one, round_two, round_three, amp, weight,
     load_sem, xs_sem, xr_sem, ys_sem, yr_sem, es_sem, er_sem, out_sem,
 ):
     nc, nn, modes, nv, nx, ny, nz = sizes
@@ -58,6 +58,9 @@
     has_y = (n > 0, n < nn - 1)
     half = nn // 2
     far_y = (n == half, n == half - 1)
+    far = jnp.logical_or(*far_y)
+    far_x = tuple(jnp.logical_and(a, far) for a in has_x)
+    near_x = tuple(jnp.logical_and(a, jnp.logical_not(far)) for a in has_x)
     near_y = tuple(jnp.logical_and(a, jnp.logical_not(b)) for a, b in zip(has_y, far_y))
     step = (-1, 1)
     zs, rest = 4, nn // 4
@@ -128,12 +131,14 @@
             src_ref=src, dst_ref=dst, send_sem=ys_sem.at[kind, way], recv_sem=yr_sem.at[kind, 1 - way],
             device_id=(c, lax.rem(n + step[way] + nn, nn)), device_id_type=MESH)
 
+    front, back = pl.ds(0, modes // 2), pl.ds(modes // 2, modes // 2)
     x_links = [
-        lambda w: x_copy(0, w, u_hbm.at[:, :, (nx - 1) * w], u.at[:, :, (nx + 1) * (1 - w)]),
+        lambda w: x_copy(0, w, u_hbm.at[front, :, (nx - 1) * w], u.at[front, :, (nx + 1) * (1 - w)]),
         lambda w: x_copy(1, w, base_hbm.at[:, (nx - 1) * w], base.at[:, (nx + 1) * (1 - w)]),
         lambda w: x_copy(2, w, sx.at[:, 1 + w], sx.at[:, 3 * (1 - w)]),
         lambda w: x_copy(3, w, field.at[0, :, 1 + (nx - 1) * w], field.at[0, :, (nx + 1) * (1 - w)]),
         lambda w: x_copy(4, w, field.at[1, :, 1 + (nx - 1) * w], field.at[1, :, (nx + 1) * (1 - w)]),
+        lambda w: x_copy(5, w, u_hbm.at[back, :, (nx - 1) * w], u.at[back, :, (nx + 1) * (1 - w)]),
     ]
     y_links = [
         lambda w: y_copy(0, w, bface.at[w], bhalo.at[1 - w]),
@@ -161,6 +166,8 @@
             @pl.when(has[w])
             def _():
                 link(w).wait_send()
+
+    send(x_links[0], far_x)
 
     pick_row = iota((2 * nx, nx * ny), 0)
     from_row = iota((2 * nx, nx * ny), 1)
@@ -273,7 +280,8 @@
     cells_all = nc * nn * nv * nx * ny * nz
     total = jnp.sum(finish(threes, round_three, 2), axis=1, keepdims=True)
     send(y_links[5], far_y)
-    send(x_links[0], has_x)
+    send(x_links[0], near_x)
+    send(x_links[5], has_x)
     send(y_links[4], near_y)
     send(y_links[5], near_y)
     send(x_links[1], has_x)
@@ -369,62 +377,67 @@
     mix_group(plane_of(0), 0, 0)
     lax.fori_loop(0, nx - 2, plane, 0)
     receive(x_links[0], has_x)
+    receive(x_links[5], has_x)
     lax.fori_loop(nx - 2, nx, plane, 0)
 
-    receive(y_links[4], has_y)
-    receive(y_links[5], has_y)
-    fterm[...] = jnp.zeros(fterm.shape, F32)
-
-    def cross_mode(m, carry):
-        for s in (0, 1):
-            fterm[s] += wface[s, m].reshape(nv, nx, nz) * uhalo[s, m].astype(F32)
-        return carry
-
-    lax.fori_loop(0, modes, cross_mode, 0)
-    receive(y_links[1], has_y)
     receive(x_links[2], has_x)
-    fterm[0] = shalo[0] - fterm[0]
-    fterm[1] = fterm[1] - shalo[1]
-
-    def add_rows(target, x0):
-        for side in (0, 1):
-            for x in range(nx):
-                end = pl.ds((ny - 1) * side, 1)
-                target[:, x + x0, end, :] = target[:, x + x0, end, :] + fterm[side, :, pl.ds(x, 1), :]
+    for j in range(nv):
+        field[0, j, 1] = weight[0] * (grad[j, 0] - (sx_all[j, 1] - sx[j, 0]))
+        field[0, j, nx] = weight[nx - 1] * (grad[j, nx - 1] - (sx[j, 3] - sx_all[j, nx - 2]))
 
     def grad_plane(x, carry):
         for j in range(nv):
-            grad[j, x] = grad[j, x] - (sx_all[j, x + 1] - sx_all[j, x - 1])
+            field[0, j, x + 1] = weight[x] * (grad[j, x] - (sx_all[j, x + 1] - sx_all[j, x - 1]))
         return carry
 
-    for j in range(nv):
-        grad[j, 0] = grad[j, 0] - (sx_all[j, 1] - sx[j, 0])
-        grad[j, nx - 1] = grad[j, nx - 1] - (sx[j, 3] - sx_all[j, nx - 2])
     lax.fori_loop(1, nx - 1, grad_plane, 0, unroll=2)
-    add_rows(grad, 0)
-
-    def apply(slot, source, target):
-        def weigh(x, carry):
-            for j in range(nv):
-                field[slot, j, x + 1] = weight[x] * source[j, x]
+    receive(y_links[4], has_y)
+    receive(y_links[1], has_y)
+
+    def cross(first_mode, last_mode):
+        def terms(j, carry):
+            for s in (0, 1):
+                value = (shalo if first_mode == 0 else fterm)[s, j]
+                value = -value if first_mode == 0 and s == 1 else value
+                for m in range(first_mode, last_mode):
+                    term = wface[s, m, pl.ds(pl.multiple_of(j * nx, nx), nx), :] * uhalo[s, m, j].astype(F32)
+                    value = value - term if s == 0 else value + term
+                fterm[s, j] = value
             return carry
 
-        lax.fori_loop(0, nx, weigh, 0, unroll=2)
+        lax.fori_loop(0, nv, terms, 0)
+
+    cross(0, GROUP)
+    receive(y_links[5], has_y)
+    cross(GROUP, modes)
+
+    def add_rows(target, x0, weighted):
+        for side in (0, 1):
+            end = pl.ds((ny - 1) * side, 1)
+            for x in range(nx):
+                change = fterm[side, :, pl.ds(x, 1), :]
+                if weighted:
+                    change = change * weight[x, end, :]
+                target[:, x + x0, end, :] = target[:, x + x0, end, :] + change
+
+    add_rows(field.at[0], 1, True)
+
+    def apply(slot):
+        target = field.at[1] if slot == 0 else grad
+        shift = 0 if slot == 0 else 1
         for side in (0, 1):
             for x in range(nx):
                 ysend[slot, side, :, pl.ds(x, 1), :] = field[slot, :, 1 + x, pl.ds((ny - 1) * side, 1), :]
+        send(y_links[2 + slot], has_y)
         send(x_links[3 + slot], has_x)
-        send(y_links[2 + slot], has_y)
-
 
         def mixed(x, carry):
             wall[x] = dot(mat2[pl.ds(0, 4 * kv), :], split3(field[slot, :, x].reshape(kv, nz)))
             return carry
 
         lax.fori_loop(1, nx + 1, mixed, 0, unroll=4)
-        own = [dot(mat2[pl.ds(4 * kv, kv), :], split3(ysend[slot, s].reshape(kv, nz))) for s in (0, 1)]
         for s in (0, 1):
-            wface[s, 0] = own[s]
+            wface[s, 0] = dot(mat2[pl.ds(4 * kv, kv), :], split3(ysend[slot, s].reshape(kv, nz)))
 
         def result_plane(x, carry):
             for j in range(nv):
@@ -434,26 +447,27 @@
                 here = base[j, x]
                 value = base[j, x + 1] * (wx - wall[x + 1, r, :]) - base[j, x - 1] * (wx - wall[x - 1, r, :])
                 value = value + base_dz[j, x - 1] * wz - diff_lanes(here * wz)
-                target[j, x - 1] = value - rows_up(here * wm) - rows_down(here * wp)
+                value = value - rows_up(here * wm) - rows_down(here * wp)
+                target[j, x - shift] = weight[x - 1] * value if slot == 0 else value
             return carry
 
         lax.fori_loop(2, nx, result_plane, 0, unroll=2)
         if slot == 0:
             receive(x_links[1], has_x)
             receive(y_links[0], has_y)
+        receive(y_links[2 + slot], has_y)
+        for s in (0, 1):
+            far_side = dot(mat2[pl.ds(4 * kv, kv), :], split3(yhalo[slot, s].reshape(kv, nz)))
+            change = (far_side - wface[s, 0]).reshape(nv, nx, nz) * bhalo[s]
+            fterm[s] = change if s == 0 else -change
         receive(x_links[3 + slot], has_x)
-        receive(y_links[2 + slot], has_y)
         for x in (0, nx + 1):
             wall[x, pl.ds(0, kv), :] = dot(mat2[pl.ds(0, kv), :], split3(field[slot, :, x].reshape(kv, nz)))
         lax.fori_loop(0, 2, lambda s, carry: result_plane(1 + (nx - 1) * s, carry), 0, unroll=2)
-        for s in (0, 1):
-            far = dot(mat2[pl.ds(4 * kv, kv), :], split3(yhalo[slot, s].reshape(kv, nz)))
-            change = (far - wface[s, 0]).reshape(nv, nx, nz) * bhalo[s]
-            fterm[s] = change if s == 0 else -change
-        add_rows(target, 0)
-
-    apply(0, grad, result)
-    apply(1, result, grad)
+        add_rows(target, 1 - shift, slot == 0)
+
+    apply(0)
+    apply(1)
     store = pltpu.make_async_copy(grad, out_hbm, out_sem)
     store.start()
     for link in x_links:
@@ -515,10 +529,9 @@
             vm((max(nn // 4 - 1, 1), modes, 128), F32),
             vm((modes, 256), F32),
             vm((nx, ny, nz), F32),
-            vm((nv, nx, ny, nz), F32),
             pltpu.SemaphoreType.DMA((2 * groups + 3,)),
-            pltpu.SemaphoreType.DMA((5, 2)),
-            pltpu.SemaphoreType.DMA((5, 2)),
+            pltpu.SemaphoreType.DMA((6, 2)),
+            pltpu.SemaphoreType.DMA((6, 2)),
             pltpu.SemaphoreType.DMA((6, 2)),
             pltpu.SemaphoreType.DMA((6, 2)),
             pltpu.SemaphoreType.DMA((nc + nn // 4 + 1,)),

time: 68.5 us -> 68.6 us (level)
  no operation moved by 1% of the time
where the time goes in v5:
time: 68.6 us; the launch traced here: 68.1 us
  Pallas kernels  65.6 us (96%)
  local copies, waits for them, and re-layouts  2.52 us (4%)
    pallas_call x1, Pallas kernels, per_device(): pl.pallas_call(functools.partial(kernel, (nc, nn, modes, nv, nx, ny, nz))...  65.6 us
    unnamed x1, local copies, waits for them, and re-layouts  2.52 us

profile of v5, /device:TPU:6, one launch (start us, length us, event | category | flops | bytes accessed | tf_op | source)
XLA Modules:
  0.0 68.1 jit_solution(11973207141307589641)
XLA Ops:
  0.0 65.6 %shard_map.64 = f32[5,16,16,256]{3,2,1,0:T(8,128)} custom-call(bf16[16,5,16,16,256]{4,3,2,1,0:T(8,128)(2,1)} %u_hbm.1, bf16[16,5,16,16,256]{4,3,2,1,0:T(8,128)(2,1)} %v_hbm.1, f32[5,16,16,256]{3,2,1,0:T(8,128)} %base_hbm.1, s32[16,16,256]{2,1,0:T(8,128)} %cell_hbm.1, f32[5,3,5]{2,1,0:T(4,128)} %bitcast.1, s32[16]{0:T(128)} %pick.1), custom_call_target="tpu_custom_call" | custom-call | tf_op jit(solution)/shard_map/pallas_call | solution.py:490
  65.6 2.5 %copy.8 = f32[5,16,16,256]{3,2,1,0:T(8,128)} copy(f32[5,16,16,256]{3,2,1,0:T(8,128)} %shard_map.64) | data formatting | bytes 2621440

commit v6 on v5

--- a/solution.py
+++ b/solution.py
@@ -58,9 +58,6 @@
     has_y = (n > 0, n < nn - 1)
     half = nn // 2
     far_y = (n == half, n == half - 1)
-    far = jnp.logical_or(*far_y)
-    far_x = tuple(jnp.logical_and(a, far) for a in has_x)
-    near_x = tuple(jnp.logical_and(a, jnp.logical_not(far)) for a in has_x)
     near_y = tuple(jnp.logical_and(a, jnp.logical_not(b)) for a, b in zip(has_y, far_y))
     step = (-1, 1)
     zs, rest = 4, nn // 4
@@ -166,8 +163,6 @@
             @pl.when(has[w])
             def _():
                 link(w).wait_send()
-
-    send(x_links[0], far_x)
 
     pick_row = iota((2 * nx, nx * ny), 0)
     from_row = iota((2 * nx, nx * ny), 1)
@@ -280,7 +275,7 @@
     cells_all = nc * nn * nv * nx * ny * nz
     total = jnp.sum(finish(threes, round_three, 2), axis=1, keepdims=True)
     send(y_links[5], far_y)
-    send(x_links[0], near_x)
+    send(x_links[0], has_x)
     send(x_links[5], has_x)
     send(y_links[4], near_y)
     send(y_links[5], near_y)
@@ -448,7 +443,7 @@
                 value = base[j, x + 1] * (wx - wall[x + 1, r, :]) - base[j, x - 1] * (wx - wall[x - 1, r, :])
                 value = value + base_dz[j, x - 1] * wz - diff_lanes(here * wz)
                 value = value - rows_up(here * wm) - rows_down(here * wp)
-                target[j, x - shift] = weight[x - 1] * value if slot == 0 else value
+                target[j, x - shift] = weight[x - 1] * value if slot == 0 else -value
             return carry
 
         lax.fori_loop(2, nx, result_plane, 0, unroll=2)
@@ -459,7 +454,7 @@
         for s in (0, 1):
             far_side = dot(mat2[pl.ds(4 * kv, kv), :], split3(yhalo[slot, s].reshape(kv, nz)))
             change = (far_side - wface[s, 0]).reshape(nv, nx, nz) * bhalo[s]
-            fterm[s] = change if s == 0 else -change
+            fterm[s] = change if s == slot else -change
         receive(x_links[3 + slot], has_x)
         for x in (0, nx + 1):
             wall[x, pl.ds(0, kv), :] = dot(mat2[pl.ds(0, kv), :], split3(field[slot, :, x].reshape(kv, nz)))
@@ -487,7 +482,7 @@
     vm = pltpu.VMEM
     any_space = pl.BlockSpec(memory_space=pl.ANY)
     smem = pl.BlockSpec(memory_space=pltpu.SMEM)
-    return pl.pallas_call(
+    negated = pl.pallas_call(
         functools.partial(kernel, (nc, nn, modes, nv, nx, ny, nz)),
         out_shape=jax.ShapeDtypeStruct(base.shape, F32),
         in_specs=[any_space] * 5 + [smem],
@@ -541,6 +536,7 @@
         compiler_params=pltpu.CompilerParams(
             collective_id=0, has_side_effects=True, vmem_limit_bytes=60 * 2**20),
     )(u, v, base, cell, mix.transpose(1, 0, 2), pick)
+    return -negated
 
 
 def solution(mesh):

time: 68.6 us -> 67.1 us (0.978)
  other arithmetic: 0 us -> 2.52 us
  local copies, waits for them, and re-layouts: 2.52 us -> 0 us
  Pallas kernels: 65.6 us -> 64.4 us
    neg x0 -> x1, other arithmetic: none -> 2.52 us  [per_device(): return -negated]
    unnamed x1 -> x0, local copies, waits for them, and re-layouts: 2.52 us -> none
    pallas_call x1, Pallas kernels: 65.6 us -> 64.4 us  [per_device(): pl.pallas_call(functools.partial(kernel, (nc, nn, modes, nv, nx, ny, nz))...]
where the time goes in v6:
time: 67.1 us; the launch traced here: 67 us
  Pallas kernels  64.4 us (96%)
  other arithmetic  2.52 us (4%)
    pallas_call x1, Pallas kernels, per_device(): pl.pallas_call(functools.partial(kernel, (nc, nn, modes, nv, nx, ny, nz))...  64.4 us
    neg x1, other arithmetic, per_device(): return -negated  2.52 us

profile of v6, /device:TPU:6, one launch (start us, length us, event | category | flops | bytes accessed | tf_op | source)
XLA Modules:
  0.0 67.0 jit_solution(15919436728407971341)
XLA Ops:
  0.0 64.4 %shard_map.64 = f32[5,16,16,256]{3,2,1,0:T(8,128)} custom-call(bf16[16,5,16,16,256]{4,3,2,1,0:T(8,128)(2,1)} %u_hbm.1, bf16[16,5,16,16,256]{4,3,2,1,0:T(8,128)(2,1)} %v_hbm.1, f32[5,16,16,256]{3,2,1,0:T(8,128)} %base_hbm.1, s32[16,16,256]{2,1,0:T(8,128)} %cell_hbm.1, f32[5,3,5]{2,1,0:T(4,128)} %bitcast.1, s32[16]{0:T(128)} %pick.1), custom_call_target="tpu_custom_call" | custom-call | tf_op jit(solution)/shard_map/pallas_call | solution.py:485
  64.5 2.5 %neg.3 = f32[5,16,16,256]{3,2,1,0:T(8,128)} negate(f32[5,16,16,256]{3,2,1,0:T(8,128)} %shard_map.64) | non-fusion elementwise | flops 327680 | bytes 2621440 | tf_op jit(solution)/shard_map/neg | solution.py:539

commit v7 on v6

--- a/solution.py
+++ b/solution.py
@@ -142,8 +142,8 @@
         lambda w: y_copy(1, w, sface.at[w], shalo.at[1 - w]),
         lambda w: y_copy(2, w, ysend.at[0, w], yhalo.at[0, 1 - w]),
         lambda w: y_copy(3, w, ysend.at[1, w], yhalo.at[1, 1 - w]),
-        lambda w: y_copy(4, w, uface.at[w, pl.ds(0, GROUP)], uhalo.at[1 - w, pl.ds(0, GROUP)]),
-        lambda w: y_copy(5, w, uface.at[w, pl.ds(GROUP, modes - GROUP)], uhalo.at[1 - w, pl.ds(GROUP, modes - GROUP)]),
+        lambda w: y_copy(4, w, uface.at[w, front], uhalo.at[1 - w, front]),
+        lambda w: y_copy(5, w, uface.at[w, back], uhalo.at[1 - w, back]),
     ]
 
     def send(link, has):
@@ -194,7 +194,7 @@
             return carry
 
         lax.fori_loop(g * GROUP, (g + 1) * GROUP, u_mode, 0)
-        if g == 0:
+        if g == groups // 2 - 1:
             send(y_links[4], far_y)
 
     def e_copy(index, peer, dst):

time: 67.1 us -> 70 us (1.043)
  Pallas kernels: 64.4 us -> 67.3 us
    pallas_call x1, Pallas kernels: 64.4 us -> 67.3 us  [per_device(): pl.pallas_call(functools.partial(kernel, (nc, nn, modes, nv, nx, ny, nz))...]
where the time goes in v7:
time: 70 us; the launch traced here: 69.9 us
  Pallas kernels  67.3 us (96%)
  other arithmetic  2.52 us (4%)
    pallas_call x1, Pallas kernels, per_device(): pl.pallas_call(functools.partial(kernel, (nc, nn, modes, nv, nx, ny, nz))...  67.3 us
    neg x1, other arithmetic, per_device(): return -negated  2.52 us

profile of v7, /device:TPU:6, one launch (start us, length us, event | category | flops | bytes accessed | tf_op | source)
XLA Modules:
  0.0 69.9 jit_solution(3609624642205811946)
XLA Ops:
  0.0 67.3 %shard_map.64 = f32[5,16,16,256]{3,2,1,0:T(8,128)} custom-call(bf16[16,5,16,16,256]{4,3,2,1,0:T(8,128)(2,1)} %u_hbm.1, bf16[16,5,16,16,256]{4,3,2,1,0:T(8,128)(2,1)} %v_hbm.1, f32[5,16,16,256]{3,2,1,0:T(8,128)} %base_hbm.1, s32[16,16,256]{2,1,0:T(8,128)} %cell_hbm.1, f32[5,3,5]{2,1,0:T(4,128)} %bitcast.1, s32[16]{0:T(128)} %pick.1), custom_call_target="tpu_custom_call" | custom-call | tf_op jit(solution)/shard_map/pallas_call | solution.py:485
  67.3 2.5 %neg.3 = f32[5,16,16,256]{3,2,1,0:T(8,128)} negate(f32[5,16,16,256]{3,2,1,0:T(8,128)} %shard_map.64) | non-fusion elementwise | flops 327680 | bytes 2621440 | tf_op jit(solution)/shard_map/neg | solution.py:539
